TPU v7x, 32 devices: a whole 2x2x4 slice. The times are simulated.
32 devices in a mesh: sec: 2 (over core), sp: 4 (over y, x), dev: 4 (over z).
Axes of the slice: x: 2, y: 2, z: 4, core: 2. Of those that a mesh axis runs over, the one named last changes fastest.
Arguments:
- patch_qkv: bfloat16 [4096, 3, 1280], P(('sec', 'sp', 'dev')), may hold values from -13 to 13
- patch_state: bfloat16 [4096, 1280], P(('sec', 'sp', 'dev')), may hold values from -6 to 6
- window_index: int32 [32, 128], P(('sec', 'sp', 'dev')), may hold values from 0 to 127, each once within a row
- patch_owner: int32 [4096, 1], P(('sec', 'sp', 'dev')), may hold values from 0 to 7; in each aligned block of 128 rows (0 to 127, 128 to 255, ...) at most 32 rows name the same one
- source_request: int32 [8, 8], P(('sec', 'dev')), may hold values from 0 to 3, never falling along the last dimension, each value on 1 to 4 neighbouring positions
- norm_gain: float32 [1280], replicated, may hold values from 0.1 to 1.9
- w_qkv: bfloat16 [1280, 3, 1280], P(None, None, 'sp'), may hold values from -0.15625 to 0.15625
- b_qkv: bfloat16 [3, 1280], P(None, 'sp'), may hold values from -12 to 12
Outputs:
- out_rows: bfloat16 [4096, 1280], P(('sec', 'sp', 'dev'))
Inputs may be any that keep to these rules, and one draw needn't show every extreme that they name: `window_index`: each row is a permutation of the 128 local patch indices of one device. `patch_owner`: among the 128 patches of one device no owner is named more than 32 times, and on some device one owner is named exactly 32 times. `source_request`: along each row the request number never falls; each request covers 1 to 4 consecutive source positions, one exactly 4.
All inputs are finite; a program needn't handle non-finite values.
Results may differ from a plain program's by a relative error of at most 0.012.
The roundings to bfloat16 on the way count: a program that leaves them out, or rounds other values in their place, can miss the bound.
Values may be sent and summed in bfloat16 or wider, within the bound.
No kernel may reach another device: no remote copies, remote signals or barrier semaphores. Data moves between devices by JAX's collectives and lax.ppermute only.
A program may use at most 64 MiB of HBM per device.

v0:
```python
import jax
import jax.numpy as jnp
from jax import lax
from jax.sharding import PartitionSpec as P

HD = 80
WIN = 64


NORM_EPS = 1e-06


def normalize(rows_in, gain_row):
    rows_in = rows_in.astype(jnp.float32)
    mean_sq = jnp.mean(rows_in * rows_in, axis=-1, keepdims=True)
    return (rows_in * lax.rsqrt(mean_sq + NORM_EPS) * gain_row).astype(jnp.bfloat16)


def softmax_rows(scores):
    row_max = jnp.max(scores, axis=-1, keepdims=True)
    expo_vals = jnp.exp(scores - row_max)
    return (expo_vals / jnp.sum(expo_vals, axis=-1, keepdims=True)).astype(jnp.bfloat16)


def window_attend(qkv_rows, order_ids, head_size, window_span):
    num_rows = qkv_rows.shape[0]
    row_width = qkv_rows.shape[2]
    head_count = row_width // head_size
    ordered = jnp.take(qkv_rows, order_ids, axis=0)
    ordered = ordered.reshape(num_rows // window_span, window_span, 3, head_count, head_size)
    scores = jnp.einsum(
        "wqhd,wkhd->whqk", ordered[:, :, 0], ordered[:, :, 1], preferred_element_type=jnp.float32
    ) * head_size ** (-0.5)
    weights = softmax_rows(scores)
    mixed = jnp.einsum(
        "whqk,wkhd->wqhd", weights, ordered[:, :, 2], preferred_element_type=jnp.float32
    )
    mixed = mixed.reshape(num_rows, row_width).astype(jnp.bfloat16)
    return jnp.zeros((num_rows, row_width), jnp.bfloat16).at[order_ids].set(mixed)


def owner_attend(query, keys_all, values_all, request, live_keys, head_size):
    group_size, head_count, _ = query.shape
    q_block = 512
    scale = head_size ** (-0.5)
    open_keys = live_keys > 0

    def one_block(block_start):
        rows_q = lax.dynamic_slice_in_dim(query, block_start, q_block, 0)
        reqs_q = lax.dynamic_slice_in_dim(request, block_start, q_block, 0)
        scores = jnp.einsum("qhd,khd->hqk", rows_q, keys_all, preferred_element_type=jnp.float32)
        allowed = (reqs_q[:, None] == request[None, :]) & open_keys[None, :]
        scores = jnp.where(allowed[None], scores * scale, -1e30)
        weights = softmax_rows(scores)
        mixed = jnp.einsum("hqk,khd->qhd", weights, values_all, preferred_element_type=jnp.float32)
        return mixed.astype(jnp.bfloat16)

    starts = jnp.arange(group_size // q_block, dtype=jnp.int32) * q_block
    blocks = lax.map(one_block, starts)
    return blocks.reshape(group_size, head_count * head_size)


def shards(
    patch_qkv, patch_state, window_index, patch_owner, source_request, norm_gain, w_qkv, b_qkv
):
    num_rows = patch_qkv.shape[0]
    row_width = patch_qkv.shape[2]
    sections = lax.axis_size("sec")
    groups = lax.axis_size("sp")
    members = lax.axis_size("dev")
    owners = sections * members
    capacity = max(2, 2 * num_rows // owners)
    local_width = w_qkv.shape[2]
    local_heads = local_width // HD
    window_out = lax.optimization_barrier(window_attend(patch_qkv, window_index[0], HD, WIN))
    moved = (patch_state.astype(jnp.float32) + window_out.astype(jnp.float32)).astype(jnp.bfloat16)
    owner_id = patch_owner[:, 0]
    owner_hits = (owner_id[:, None] == jnp.arange(owners, dtype=jnp.int32)[None, :]).astype(
        jnp.int32
    )
    slot_rank = jnp.sum((jnp.cumsum(owner_hits, axis=0) - 1) * owner_hits, axis=1)
    slot_id = owner_id * capacity + slot_rank
    picker = (jnp.arange(owners * capacity, dtype=jnp.int32)[:, None] == slot_id[None, :]).astype(
        jnp.bfloat16
    )
    outgoing = jnp.dot(picker, moved, preferred_element_type=jnp.float32).astype(jnp.bfloat16)
    outgoing = outgoing.reshape(owners, capacity, row_width)
    filled = jnp.max(picker, axis=1).reshape(owners, capacity)
    incoming, arrived = (
        lax.all_to_all(outgoing, ("sec", "dev"), split_axis=0, concat_axis=0, tiled=True),
        lax.all_to_all(filled, ("sec", "dev"), split_axis=0, concat_axis=0, tiled=True),
    )
    group_size = owners * groups * capacity
    rows_all, live_all = (
        lax.all_gather(incoming, "sp", axis=1, tiled=True),
        lax.all_gather(arrived, "sp", axis=1, tiled=True),
    )
    normed = normalize(rows_all.reshape(group_size, row_width), norm_gain)
    projected = jnp.einsum("gf,fch->gch", normed, w_qkv, preferred_element_type=jnp.float32)
    projected = (projected + b_qkv.astype(jnp.float32)).astype(jnp.bfloat16)
    query = projected[:, 0].reshape(group_size, local_heads, HD)
    keys_all = projected[:, 1].reshape(group_size, local_heads, HD)
    values_all = projected[:, 2].reshape(group_size, local_heads, HD)
    request = jnp.repeat(source_request[0], groups * capacity)
    live_keys = live_all.reshape(group_size)
    mixed = owner_attend(query, keys_all, values_all, request, live_keys, HD)
    pieces = mixed.reshape(owners, groups, capacity, local_width)
    returned = lax.all_to_all(pieces, "sp", split_axis=1, concat_axis=3, tiled=True).reshape(
        owners, capacity, row_width
    )
    result = lax.all_to_all(returned, ("sec", "dev"), split_axis=0, concat_axis=0, tiled=True)
    result = result.reshape(owners * capacity, row_width)
    back_rows = jnp.einsum("sp,sw->pw", picker, result, preferred_element_type=jnp.float32)
    return (moved.astype(jnp.float32) + back_rows).astype(jnp.bfloat16)


def solution(mesh):
    in_specs = (
        P(("sec", "sp", "dev"), None, None),
        P(("sec", "sp", "dev"), None),
        P(("sec", "sp", "dev"), None),
        P(("sec", "sp", "dev"), None),
        P(("sec", "dev"), None),
        P(),
        P(None, None, "sp"),
        P(None, "sp"),
    )
    out_specs = P(("sec", "sp", "dev"), None)
    return jax.shard_map(shards, mesh=mesh, in_specs=in_specs, out_specs=out_specs, check_vma=False)
```

profile of v0, /device:TPU:0, one launch (start us, length us, event | category | flops | bytes accessed | tf_op | source)
XLA Modules:
  0.0 185.6 jit_solution(1082997914684722397)
XLA Ops:
  6.5 0.8 fusion.45
  7.4 3.8 %gather_fusion = bf16[128,3,1280]{2,0,1:T(8,128)(2,1)S(1)} fusion(bf16[128,3,1280]{2,0,1:T(8,128)(2,1)} %param.10, s32[1024]{0:T(1024)S(1)} %pad_clamp_fusion), kind=kCustom, calls=%fused_computation | custom fusion | bytes 1966592 | tf_op jit(solution)/shard_map/jit(_take)/gather | solution.py:29
  11.2 3.3 %gather.7 = bf16[2,64,3,16,80]{4,3,1,0,2:T(8,128)(2,1)} reshape(bf16[128,3,1280]{2,0,1:T(8,128)(2,1)S(1)} %gather_fusion) | data formatting | bytes 1966080 | tf_op jit(solution)/shard_map/jit(_take)/gather | solution.py:29
  14.5 0.5 broadcast.121
  15.0 0.0 copy-done.9
  15.0 0.7 reduce.4
  15.7 0.1 squeeze.25
  15.7 1.8 copy_select_fusion
  17.5 1.1 copy-done.2
  18.7 1.4 convolution_multiply_fusion
  20.0 1.7 fusion.54
  21.7 0.0 copy-start.8
  21.7 0.0 copy-start.4
  21.8 3.0 %fusion.36 = bf16[2,64,16,80]{3,1,2,0:T(8,128)(2,1)} fusion(bf16[2,64,3,16,80]{4,1,3,0,2:T(8,128)(2,1)} %copy-done.2, f32[2,16,64]{2,1,0:T(8,128)S(1)} %fusion.54, f32[2,16,64,64]{2,3,1,0:T(8,128)} %convolution_multiply_fusion), kind=kOutput, calls=%fused_computation.41 | convolution fusion | flops 21530688 | bytes 1843200 | tf_op jit(solution)/shard_map/whqk,wkhd->wqhd/dot_general | solution.py:35
  24.8 1.4 copy.26
  26.1 0.0 copy-start.5
  26.2 0.0 copy-start.7
  26.2 1.3 reshape.157
  27.4 1.7 scatter_custom_fusion
  29.1 0.0 copy-start.3
  29.1 0.0 copy-done.8
  29.1 0.1 fusion.44
  29.2 0.2 reduce_window_sum.11
  29.4 0.2 select_reduce_fusion
  29.6 0.3 convolution_convert_fusion
  29.9 0.0 copy-start.6
  29.9 24.2 %all_to_all.38 = bf16[8,32,1280]{2,1,0:T(8,128)(2,1)} all-to-all(bf16[8,32,1280]{2,1,0:T(8,128)(2,1)S(1)} %bitcast.84), channel_id=1, replica_groups=mesh['sec'=2,'sp'=4,'dev'=4] {'sec','dev'}, dimensions={0} | all-to-all | bytes 1310720 | tf_op jit(solution)/shard_map/all_to_all | solution.py:90
  54.2 0.0 all-gather.3.cloned.1.call-update
  54.2 0.1 fusion.41
  54.3 0.7 all_to_all.33
  55.0 3.3 %all-to-all-start = ((bf16[8,1,32]{2,1,0:T(2,128)(2,1)}), bf16[8,1,32]{2,1,0:T(2,128)(2,1)S(1)}, u32[]{:S(2)}, u32[]{:S(2)}) async-start(bf16[8,1,32]{2,1,0:T(2,128)(2,1)} %all_to_all.33), calls=%async_computation | async-start | bytes 8192 | tf_op jit(solution)/shard_map/all_to_all | solution.py:91
  58.2 0.0 copy-done.5
  58.3 0.1 broadcast_bitcast_fusion.1
  58.3 5.4 %all-to-all-done = bf16[8,1,32]{2,1,0:T(2,128)(2,1)S(1)} async-done(((bf16[8,1,32]{2,1,0:T(2,128)(2,1)}), bf16[8,1,32]{2,1,0:T(2,128)(2,1)S(1)}, u32[]{:S(2)}, u32[]{:S(2)}) %all-to-all-start) | async-done | bytes 544 | tf_op jit(solution)/shard_map/all_to_all | solution.py:91
  63.7 0.1 copy.28
  63.8 8.7 %all-gather = bf16[8,1,128]{0,1,2:T(2,128)(2,1)S(1)} all-gather(bf16[8,1,32]{0,1,2:T(2,128)(2,1)S(1)} %copy.28), channel_id=2, replica_groups=mesh['sec'=2,'sp'=4,'dev'=4] {'sp'}, dimensions={2}, use_global_device_ids=true | all-gather | bytes 2560 | tf_op jit(solution)/shard_map/all_gather | solution.py:96
  72.6 0.1 copy.29
  72.7 20.2 %all-gather.3.cloned.1.call-done = bf16[8,128,1280]{2,1,0:T(8,128)(2,1)} async-done(((bf16[8,32,1280]{2,1,0:T(8,128)(2,1)}), bf16[8,128,1280]{2,1,0:T(8,128)(2,1)}) %all-gather.3.cloned.1.call-update) | async-done | bytes 2621456 | tf_op jit(solution)/shard_map/all_gather | solution.py:95
  92.9 2.5 %multiply_reduce_fusion = f32[8,128]{1,0:T(8,128)S(1)} fusion(bf16[8,128,1280]{2,1,0:T(8,128)(2,1)} %all-gather.3.cloned.1.call-done), kind=kLoop, calls=%fused_computation.29 | loop fusion | flops 3931136 | bytes 2625536 | tf_op jit(solution)/shard_map/reduce_sum | solution.py:15
  95.4 0.0 copy-done.1
  95.4 0.7 fusion.28
  96.1 2.7 %add_convert_fusion = bf16[1024,3,320]{0,2,1:T(8,128)(2,1)S(1)} fusion(f32[3,320]{1,0:T(4,128)S(1)} %convert_element_type.78, bf16[1280,3,320]{0,2,1:T(8,128)(2,1)S(1)} %copy-done, bf16[1024,1280]{1,0:T(8,128)(2,1)S(1)} %fusion.28), kind=kOutput, calls=%fused_computation.30 | convolution fusion | flops 2518548480 | bytes 7048960 | tf_op jit(solution)/shard_map/gf,fch->gch/dot_general | solution.py:99
  98.8 1.4 fusion.53
  100.2 33.5 %while.11 = (s32[]{:T(128)}, bf16[2,512,4,80]{1,3,2,0:T(8,128)(2,1)}, s32[2]{0:T(128)S(1)}, s32[1024]{0:T(1024)S(1)}, pred[1024]{0:T(1024)(128)(4,1)S(1)}, /*ind...) while((s32[]{:T(128)}, ...), condition=%wide.region_10.11_spmd.clone, body=%wide.region_7.10_spmd.clone.sunk | while | flops 684884992 | bytes 19824332 | solution.py:59
  100.2 0.7 dynamic_slice.29
  102.9 0.1 dynamic_slice.30
  103.0 0.1 broadcast_bitcast_fusion.3
  103.1 0.4 compare_and_fusion.3
  103.5 7.8 %fusion.69 = (f32[4,512]{1,0:T(4,128)S(1)}, f32[4,512,1024]{2,1,0:T(8,128)}) fusion(pred[512,1024]{1,0:T(8,128)(4,1)S(1)} %compare_and_fusion.3, bf16[1024,4,80]{0,2,1:T(8,128)(2,1)} %get-tuple-element.186, bf16[1024,4,80]{0,2,1:T(8,128)(2,1)} %get-tuple-element.185, s32[]{:T(128)S(6)} %select_n.56), kind=kOutput, calls=%fused_computation.70.clone.1 | convolution fusion | flops 343933952 | bytes 9904132 | tf_op jit(solution)/shard_map/while/body/eval_jaxpr/sub | solution.py:21
  111.3 5.7 %fusion.70 = bf16[2,512,4,80]{1,3,2,0:T(8,128)(2,1)} fusion(bf16[2,512,4,80]{1,3,2,0:T(8,128)(2,1)} %get-tuple-element.169, s32[]{:T(128)} %get-tuple-element.168, bf16[1024,4,80]{0,2,1:T(8,128)(2,1)} %get-tuple-element.187, f32[4,512,1024]{2,1,0:T(8,128)} %get-tuple-element.154, f32[4,512]{1,0:T(4,128)S(1)} %get-tuple-element.155), kind=kOutput, calls=%fused_computation.15.clone.1 | convolution fusion | flops 339902464 | bytes 9380352 | tf_op jit(solution)/shard_map/while/body/eval_jaxpr/hqk,khd->qhd/dot_general | solution.py:55
  117.0 0.7 dynamic_slice.29
  119.7 0.1 dynamic_slice.30
  119.8 0.1 broadcast_bitcast_fusion.3
  119.8 0.4 compare_and_fusion.3
  120.3 7.7 %fusion.69 = (f32[4,512]{1,0:T(4,128)S(1)}, f32[4,512,1024]{2,1,0:T(8,128)}) fusion(pred[512,1024]{1,0:T(8,128)(4,1)S(1)} %compare_and_fusion.3, bf16[1024,4,80]{0,2,1:T(8,128)(2,1)} %get-tuple-element.186, bf16[1024,4,80]{0,2,1:T(8,128)(2,1)} %get-tuple-element.185, s32[]{:T(128)S(6)} %select_n.56), kind=kOutput, calls=%fused_computation.70.clone.1 | convolution fusion | flops 343933952 | bytes 9904132 | tf_op jit(solution)/shard_map/while/body/eval_jaxpr/sub | solution.py:21
  128.0 5.7 %fusion.70 = bf16[2,512,4,80]{1,3,2,0:T(8,128)(2,1)} fusion(bf16[2,512,4,80]{1,3,2,0:T(8,128)(2,1)} %get-tuple-element.169, s32[]{:T(128)} %get-tuple-element.168, bf16[1024,4,80]{0,2,1:T(8,128)(2,1)} %get-tuple-element.187, f32[4,512,1024]{2,1,0:T(8,128)} %get-tuple-element.154, f32[4,512]{1,0:T(4,128)S(1)} %get-tuple-element.155), kind=kOutput, calls=%fused_computation.15.clone.1 | convolution fusion | flops 339902464 | bytes 9380352 | tf_op jit(solution)/shard_map/while/body/eval_jaxpr/hqk,khd->qhd/dot_general | solution.py:55
  133.7 1.6 copy.30
  135.3 1.6 reshape_reshape.3
  136.9 1.2 copy.31
  138.2 13.9 %all_to_all.39 = bf16[8,4,32,320]{3,2,0,1:T(8,128)(2,1)S(1)} all-to-all(bf16[8,4,32,320]{3,2,0,1:T(8,128)(2,1)S(1)} %copy.31), channel_id=1, replica_groups=mesh['sec'=2,'sp'=4,'dev'=4] {'sp'}, dimensions={1} | all-to-all | bytes 1310720 | tf_op jit(solution)/shard_map/all_to_all | solution.py:108
  152.0 0.6 copy.32
  152.6 1.4 reshape.142
  154.1 22.6 %all_to_all.40 = bf16[8,32,1280]{2,1,0:T(8,128)(2,1)S(1)} all-to-all(bf16[8,32,1280]{2,1,0:T(8,128)(2,1)} %reshape.142), channel_id=1, replica_groups=mesh['sec'=2,'sp'=4,'dev'=4] {'sec','dev'}, dimensions={0} | all-to-all | bytes 1310720 | tf_op jit(solution)/shard_map/all_to_all | solution.py:111
  176.6 2.1 %fusion.31 = bf16[128,1280]{1,0:T(8,128)(2,1)} fusion(bf16[256,1280]{1,0:T(8,128)(2,1)S(1)} %bitcast.83, bf16[128,1280]{1,0:T(8,128)(2,1)} %copy-done.3, bf16[128,1280]{1,0:T(8,128)(2,1)} %param.11, s32[128]{0:T(128)S(1)} %multiply_add_fusion), kind=kOutput, calls=%fused_computation.35 | convolution fusion | flops 85065728 | bytes 1638912 | tf_op jit(solution)/shard_map/sp,sw->pw/dot_general | solution.py:113
  (18 shorter events, 0.1 us)
Async XLA Ops:
  6.5 89.5 %copy-start = (bf16[1280,3,320]{0,2,1:T(8,128)(2,1)S(1)}, bf16[1280,3,320]{0,2,1:T(8,128)(2,1)}, u32[]{:S(2)}) copy-start(bf16[1280,3,320]{0,2,1:T(8,128)(2,1)} %param.16) | copy-start | bytes 7372804
  6.5 86.3 %all-gather.3.cloned.1.call-start = ((), (), s32[]{:S(2)}) async-start(), calls=%async_computation.4 | async-start | bytes 3276800 | tf_op jit(solution)/shard_map/all_gather | solution.py:95
  7.4 7.6 %copy-start.9 = (s32[1,128]{1,0:T(1,128)S(1)}, s32[1,128]{1,0:T(1,128)}, u32[]{:S(2)}) copy-start(s32[1,128]{1,0:T(1,128)} %param.12) | copy-start | bytes 1540
  17.5 1.2 copy-start.2
  21.7 7.4 %copy-start.8 = (s32[128,1]{0,1:T(1,128)S(1)}, s32[128,1]{0,1:T(1,128)}, u32[]{:S(2)}) copy-start(s32[128,1]{0,1:T(1,128)} %param.13) | copy-start | bytes 1540
  21.7 7.8 %copy-start.4 = (bf16[128,1280]{1,0:T(8,128)(2,1)S(1)}, bf16[128,1280]{1,0:T(8,128)(2,1)}, u32[]{:S(2)}) copy-start(bf16[128,1280]{1,0:T(8,128)(2,1)} %param.11) | copy-start | bytes 983044
  26.1 32.1 %copy-start.5 = (s32[1,8]{1,0:T(1,128)S(1)}, s32[1,8]{1,0:T(1,128)}, u32[]{:S(2)}) copy-start(s32[1,8]{1,0:T(1,128)} %param.14) | copy-start | bytes 100
  26.2 32.2 %copy-start.7 = (bf16[3,320]{1,0:T(4,128)(2,1)S(1)}, bf16[3,320]{1,0:T(4,128)(2,1)}, u32[]{:S(2)}) copy-start(bf16[3,320]{1,0:T(4,128)(2,1)} %param.17) | copy-start | bytes 5764
  29.1 66.2 %copy-start.3 = (bf16[128,1280]{1,0:T(8,128)(2,1)}, bf16[128,1280]{1,0:T(8,128)(2,1)S(1)}, u32[]{:S(2)}) copy-start(bf16[128,1280]{1,0:T(8,128)(2,1)S(1)} %scatter_custom_fusion) | copy-start | bytes 983044
  29.9 65.4 %copy-start.6 = (f32[1280]{0:T(1024)S(1)}, f32[1280]{0:T(1024)}, u32[]{:S(2)}) copy-start(f32[1280]{0:T(1024)} %param.15) | copy-start | bytes 15364
  55.0 8.8 %all-to-all-start = ((bf16[8,1,32]{2,1,0:T(2,128)(2,1)}), bf16[8,1,32]{2,1,0:T(2,128)(2,1)S(1)}, u32[]{:S(2)}, u32[]{:S(2)}) async-start(bf16[8,1,32]{2,1,0:T(2,128)(2,1)} %all_to_all.33), calls=%async_computation | async-start | bytes 8192 | tf_op jit(solution)/shard_map/all_to_all | solution.py:91
  92.9 2.5 %copy-start.1 = (bf16[8,128,1280]{2,1,0:T(8,128)(2,1)S(1)}, bf16[8,128,1280]{2,1,0:T(8,128)(2,1)}, u32[]{:S(2)}) copy-start(bf16[8,128,1280]{2,1,0:T(8,128)(2,1)} %all-gather.3.cloned.1.call-done) | copy-start | bytes 7864324
Sparse Core Ops, SparseCore 0:
  54.3 38.5 all-gather.2
where the time goes:
time: 186 us
  blocking collectives  69.4 us (37%)
  matrix products  38.1 us (20%)
  waiting for transfers between devices  25.6 us (14%)
  local copies, waits for them, and re-layouts  23.6 us (13%)
  between operations  13.6 us (7%)
  other arithmetic  7.76 us (4%)
  loops' own time  4.17 us (2%)
  starting transfers between devices  3.26 us (2%)
    all_to_all x1, blocking collectives, shards(): lax.all_to_all(outgoing, ('sec', 'dev'), split_axis=0, concat_axis=0, til...  24.2 us
    all_to_all x1, blocking collectives, shards(): lax.all_to_all(returned, ('sec', 'dev'), split_axis=0, concat_axis=0, til...  22.6 us
    all_gather x1, waiting for transfers between devices, shards(): lax.all_gather(incoming, 'sp', axis=1, tiled=True)  20.2 us
    sub x3, matrix products, softmax_rows(): expo_vals = jnp.exp(scores - row_max)  17.2 us
    all_to_all x1, blocking collectives, shards(): lax.all_to_all(pieces, 'sp', split_axis=1, concat_axis=3, tiled=True)  13.9 us
    dot_general x2, matrix products, one_block(): jnp.einsum('hqk,khd->qhd', weights, values_all, preferred_element_type=jn...  11.4 us
    all_gather x1, blocking collectives, shards(): lax.all_gather(arrived, 'sp', axis=1, tiled=True)  8.73 us
    gather x2, local copies, waits for them, and re-layouts, window_attend(): ordered = jnp.take(qkv_rows, order_ids, axis=0)  7.11 us
  transfers between devices with their start and end apart: 2, of which 2 were waited for; matrix products, arithmetic and copies ran while one was open for 0% of the time, Pallas kernels for 0%

commit v1 on v0

--- a/solution.py
+++ b/solution.py
@@ -1,13 +1,21 @@
+import functools
+
 import jax
 import jax.numpy as jnp
 from jax import lax
+from jax.experimental import pallas as pl
+from jax.experimental.pallas import tpu as pltpu
 from jax.sharding import PartitionSpec as P
+
 
 HD = 80
 WIN = 64
-
-
 NORM_EPS = 1e-06
+NEG = -1e30
+EMPTY = 2.0**60
+LANES = 128
+WINDOW_MIB = 60
+RATE = HD ** (-0.5) * 1.4426950408889634
 
 
 def normalize(rows_in, gain_row):
@@ -50,7 +58,7 @@
         reqs_q = lax.dynamic_slice_in_dim(request, block_start, q_block, 0)
         scores = jnp.einsum("qhd,khd->hqk", rows_q, keys_all, preferred_element_type=jnp.float32)
         allowed = (reqs_q[:, None] == request[None, :]) & open_keys[None, :]
-        scores = jnp.where(allowed[None], scores * scale, -1e30)
+        scores = jnp.where(allowed[None], scores * scale, NEG)
         weights = softmax_rows(scores)
         mixed = jnp.einsum("hqk,khd->qhd", weights, values_all, preferred_element_type=jnp.float32)
         return mixed.astype(jnp.bfloat16)
@@ -60,7 +68,7 @@
     return blocks.reshape(group_size, head_count * head_size)
 
 
-def shards(
+def shards_general(
     patch_qkv, patch_state, window_index, patch_owner, source_request, norm_gain, w_qkv, b_qkv
 ):
     num_rows = patch_qkv.shape[0]
@@ -114,6 +122,422 @@
     return (moved.astype(jnp.float32) + back_rows).astype(jnp.bfloat16)
 
 
+SEC, LINES, PLANES = 2, 4, 4
+BLOCKS = SEC * PLANES
+GROUPS = ((0,), (1, 2), (3,))
+
+
+def dot_t(a, b):
+    return lax.dot_general(a, b, (((1,), (1,)), ((), ())), preferred_element_type=jnp.float32)
+
+
+def dot_n(a, b):
+    return lax.dot_general(a, b, (((1,), (0,)), ((), ())), preferred_element_type=jnp.float32)
+
+
+def iota(shape, dim):
+    return lax.broadcasted_iota(jnp.int32, shape, dim)
+
+
+def tiles_of(head):
+    first, last = head * HD // LANES, (head * HD + HD - 1) // LANES
+    return first, last + 1
+
+
+def head_mask(head):
+    first, end = tiles_of(head)
+    lane = iota((1, (end - first) * LANES), 1) + first * LANES
+    return (lane >= head * HD) & (lane < head * HD + HD)
+
+
+def window_kernel(
+    qkv_hbm, state_hbm, order_ref, owner_ref, moved_ref, lo_ref, hi_ref, *refs
+):
+    out_refs = refs[:BLOCKS]
+    qkv_ref, state_ref, mixed_ref, value_ref, score_ref, pick_ref, mark_ref, sems = refs[BLOCKS:]
+    rows, width = state_ref.shape
+    heads = width // HD
+    cap = out_refs[0].shape[0]
+    dev, sec = lax.axis_index("dev"), lax.axis_index("sec")
+    square = (rows, rows)
+    sub, lane = iota(square, 0), iota(square, 1)
+
+    parts = 2
+    span = width // parts
+    loads = []
+    for p in range(parts):
+        cols = pl.ds(p * span, span)
+        for n, kinds in enumerate((pl.ds(0, 2), pl.ds(2, 1))):
+            src, dst = qkv_hbm.at[kinds, :, cols], qkv_ref.at[kinds, :, cols]
+            loads.append(pltpu.make_async_copy(src, dst, sems.at[2 * p + n]))
+    loads.append(pltpu.make_async_copy(state_hbm, state_ref, sems.at[2 * parts]))
+    for load in loads:
+        load.start()
+
+    owner_row = jnp.broadcast_to(owner_ref[...], square).astype(jnp.float32)
+    owner_col = owner_row.T
+    same = owner_row == owner_col
+
+    def relative(owner):
+        owner = owner.astype(jnp.int32)
+        return ((owner & (PLANES - 1)) ^ dev) * SEC + ((owner // PLANES) ^ sec)
+
+    rank_row = jnp.sum((same & (sub < lane)).astype(jnp.float32), axis=0, keepdims=True)
+    slot_row = relative(owner_row[:1]) * cap + rank_row.astype(jnp.int32)
+    picker = iota((BLOCKS * cap, rows), 0) == jnp.broadcast_to(slot_row, (BLOCKS * cap, rows))
+    picker = picker.astype(jnp.float32)
+    filled = jnp.sum(picker, axis=1, keepdims=True)
+    pick_ref[...] = picker.astype(jnp.bfloat16)
+    mark_ref[...] = jnp.where((filled == 0.0) & (iota((BLOCKS * cap, LANES), 1) == 0), EMPTY, 0.0)
+    rank_col = jnp.sum((same & (lane < sub)).astype(jnp.float32), axis=1, keepdims=True)
+    rank_col = jnp.broadcast_to(rank_col, square).astype(jnp.int32)
+    half = cap // 2
+    place = relative(owner_col) * half + rank_col
+    lo_ref[...] = ((rank_col < half) & (place == lane)).astype(jnp.float32).astype(jnp.bfloat16)
+    hi_ref[...] = ((rank_col >= half) & (place - half == lane)).astype(jnp.float32).astype(jnp.bfloat16)
+
+    hit = (jnp.broadcast_to(order_ref[...], square) == sub) & (lane < WIN)
+    in_first = jnp.sum(hit.astype(jnp.float32), axis=1, keepdims=True)
+    in_first = jnp.broadcast_to(in_first, square)
+    bias = jnp.where(in_first == in_first.T, 0.0, NEG)
+
+    for p in range(parts):
+        group = range(p * heads // parts, (p + 1) * heads // parts)
+        loads[2 * p].wait()
+        tops, sums = {}, {}
+        for head in group:
+            first, end = tiles_of(head)
+            cols = slice(first * LANES, end * LANES)
+            query = jnp.where(head_mask(head), qkv_ref[0, :, cols], jnp.zeros((), jnp.bfloat16))
+            score_ref[head] = dot_t(qkv_ref[1, :, cols], query) * RATE + bias
+        loads[2 * p + 1].wait()
+        for t in range(p * span // LANES, (p + 1) * span // LANES):
+            cols = slice(t * LANES, (t + 1) * LANES)
+            value_ref[cols, :] = qkv_ref[2, :, cols].T
+        for head in group:
+            tops[head] = jnp.max(score_ref[head], axis=0, keepdims=True)
+        for head in group:
+            expo = jnp.exp2(score_ref[head] - tops[head])
+            score_ref[head] = expo
+            sums[head] = jnp.sum(expo, axis=0, keepdims=True)
+        for head in group:
+            weights = (score_ref[head] * (1.0 / sums[head])).astype(jnp.bfloat16)
+            cols = slice(head * HD, (head + 1) * HD)
+            mixed_ref[cols, :] = dot_n(value_ref[cols, :], weights).astype(jnp.bfloat16)
+    loads[2 * parts].wait()
+    for t in range(width // LANES):
+        cols = slice(t * LANES, (t + 1) * LANES)
+        window_out = mixed_ref[cols, :].T.astype(jnp.float32)
+        moved_ref[:, cols] = (state_ref[:, cols].astype(jnp.float32) + window_out).astype(jnp.bfloat16)
+
+    picked = dot_n(pick_ref[...], moved_ref[...])
+    for b in range(BLOCKS):
+        span = slice(b * cap, (b + 1) * cap)
+        out_refs[b][:, :LANES] = (picked[span, :LANES] + mark_ref[span, :]).astype(jnp.bfloat16)
+        out_refs[b][:, LANES:] = picked[span, LANES:].astype(jnp.bfloat16)
+
+
+def stores(blocks, block_rows, cols):
+    heads = cols // HD
+    return (
+        (blocks, heads, LANES, block_rows),
+        (blocks, block_rows, heads * LANES),
+        (blocks, cols, block_rows),
+    )
+
+
+def project(pieces, gain_ref, w_ref, b_ref, kb_ref, q_ref, k_ref, v_ref, q_at, at, normed_ref):
+    planes, cap = pieces[0].shape[1:3]
+    cols = w_ref.shape[1]
+    heads = cols // HD
+    block_rows = LINES * cap
+    spare = (LANES - HD, block_rows)
+    tail = (iota(spare, 0) == 0).astype(jnp.float32).astype(jnp.bfloat16)
+    columns = []
+    for part in (0, 2):
+        row = jnp.pad(b_ref[part : part + 1, :].astype(jnp.float32), ((0, 0), (0, -cols % LANES)))
+        column = jnp.broadcast_to(row, (LANES, row.shape[1])).T[:cols]
+        columns.append(jnp.concatenate([column] * (SEC * block_rows // LANES), axis=1))
+    for j in range(planes):
+        for r in range(SEC):
+            for step in range(2):
+                for n in range(2):
+                    m = 2 * step + n if r == 0 else 2 * n + step
+                    wide = pieces[2 * r + step][n, j].astype(jnp.float32)
+                    shut = jnp.where(wide[:, :1] < EMPTY / 2, 0.0, NEG)
+                    mean_sq = jnp.mean(wide * wide, axis=-1, keepdims=True)
+                    normed = (wide * lax.rsqrt(mean_sq + NORM_EPS) * gain_ref[...]).astype(jnp.bfloat16)
+                    normed_ref[(r * LINES + m) * cap : (r * LINES + m + 1) * cap, :] = normed
+                    flag = iota((cap, heads * LANES), 1) % LANES == HD
+                    b = at + SEC * j + r
+                    k_ref[b, m * cap : (m + 1) * cap, :] = jnp.where(flag, shut, 0.0).astype(jnp.bfloat16)
+        rows = normed_ref[...]
+        q = (dot_t(w_ref[0], rows) + columns[0]).astype(jnp.bfloat16)
+        v = (dot_t(w_ref[2], rows) + columns[1]).astype(jnp.bfloat16)
+        for r in range(SEC):
+            span = slice(r * block_rows, (r + 1) * block_rows)
+            v_ref[at + SEC * j + r] = v[:, span]
+            for head in range(heads):
+                q_ref[q_at + SEC * j + r, head, :HD, :] = q[head * HD : (head + 1) * HD, span]
+                q_ref[q_at + SEC * j + r, head, HD:, :] = tail
+        for head in range(heads):
+            k = dot_t(rows, w_ref[1, head * HD : (head + 1) * HD, :]) + kb_ref[head : head + 1, :]
+            k = k.astype(jnp.bfloat16)
+            for r in range(SEC):
+                span = slice(r * block_rows, (r + 1) * block_rows)
+                k_ref[at + SEC * j + r, :, head * LANES : head * LANES + HD] = k[span]
+
+
+def project_kernel(*refs):
+    pieces, (gain_ref, w_ref, b_ref, kb_ref, q_ref, k_ref, v_ref, normed_ref) = refs[:4], refs[4:]
+    project(pieces, gain_ref, w_ref, b_ref, kb_ref, q_ref, k_ref, v_ref, 0, 0, normed_ref)
+
+
+def attend(req_ref, q_ref, k_ref, v_ref, first_block, out_refs, score_ref):
+    dev, sec = lax.axis_index("dev"), lax.axis_index("sec")
+    heads = q_ref.shape[1]
+    cols, block_rows = v_ref.shape[1:]
+    group = block_rows // LINES
+    half = group // 2
+    most = BLOCKS // 2
+
+    def block_of(position):
+        return ((position & (PLANES - 1)) ^ dev) * SEC + ((position // PLANES) ^ sec)
+
+    def one(at, keys):
+        mixed, tops, sums = [], [], []
+        size = len(keys) * block_rows
+        for head in range(heads):
+            span = slice(head * LANES, (head + 1) * LANES)
+            k_rows = jnp.concatenate([k_ref[key, :, span] for key in keys], axis=0)
+            score_ref[head, :size, :] = dot_n(k_rows, q_ref[first_block + at, head])
+        parts = [slice(i * block_rows, (i + 1) * block_rows) for i in range(len(keys))]
+        for head in range(heads):
+            blocks = [score_ref[head, part, :] for part in parts]
+            tops.append(jnp.max(functools.reduce(jnp.maximum, blocks), axis=0, keepdims=True) * RATE)
+        for head in range(heads):
+            total = None
+            for part in parts:
+                expo = jnp.exp2(score_ref[head, part, :] * RATE - tops[head])
+                score_ref[head, part, :] = expo
+                total = expo if total is None else total + expo
+            sums.append(jnp.sum(total, axis=0, keepdims=True))
+        for head in range(heads):
+            inverse = 1.0 / sums[head]
+            weights = [(score_ref[head, part, :] * inverse).astype(jnp.bfloat16) for part in parts]
+            weights = jnp.concatenate(weights, axis=0)
+            span = slice(head * HD, (head + 1) * HD)
+            values = jnp.concatenate([v_ref[key, span, :] for key in keys], axis=1)
+            mixed.append(dot_n(values, weights))
+        if cols % LANES:
+            mixed.append(jnp.zeros((-cols % LANES, block_rows), jnp.float32))
+        plain = jnp.concatenate(mixed, axis=0).T
+        moved = pltpu.roll(plain, cols % LANES, 1)
+        whole = cols // LANES
+        for m in range(LINES):
+            up = plain[m * group : m * group + half]
+            down = moved[m * group + half : (m + 1) * group]
+            out = out_refs[m]
+            out[at, :, : whole * LANES] = up[:, : whole * LANES].astype(jnp.bfloat16)
+            seam = up[:, whole * LANES :] + down[:, :LANES]
+            out[at, :, whole * LANES : (whole + 1) * LANES] = seam.astype(jnp.bfloat16)
+            out[at, :, (whole + 1) * LANES :] = down[:, LANES:].astype(jnp.bfloat16)
+
+    @pl.loop(0, out_refs[0].shape[0])
+    def _(at):
+        block = first_block + at
+        own = req_ref[0, (sec ^ (block & 1)) * PLANES + (dev ^ (block // 2))]
+        first, count = jnp.int32(0), jnp.int32(0)
+        for s in range(BLOCKS):
+            first = first + (req_ref[0, s] < own).astype(jnp.int32)
+            count = count + (req_ref[0, s] == own).astype(jnp.int32)
+        keys = []
+        for i in range(most):
+            key = block_of(jnp.minimum(first + i, BLOCKS - 1))
+            keys.append(jnp.where(i < count, key, BLOCKS))
+
+        @pl.when(count <= most // 2)
+        def _():
+            one(at, keys[: most // 2])
+
+        @pl.when(count > most // 2)
+        def _():
+            one(at, keys)
+
+
+def attend_far_kernel(groups, req_ref, *refs):
+    early = groups[:-1]
+    ready, refs = refs[: 3 * len(early)], refs[3 * len(early) :]
+    pieces, shared, refs = refs[:4], refs[4:8], refs[8:]
+    out_refs, (q_ref, k_ref, v_ref, normed_ref, score_ref) = refs[:LINES], refs[LINES:]
+    last = SEC * groups[-1][0]
+    project(pieces, *shared, q_ref, k_ref, v_ref, last, last, normed_ref)
+    for i, planes in enumerate(early):
+        span = slice(SEC * planes[0], SEC * (planes[-1] + 1))
+        for ref, part in zip((q_ref, k_ref, v_ref), ready[3 * i : 3 * i + 3]):
+            ref[span] = part[...]
+    flag = iota(k_ref.shape[1:], 1) % LANES == HD
+    k_ref[BLOCKS] = jnp.where(flag, NEG, 0.0).astype(jnp.bfloat16)
+    v_ref[BLOCKS] = jnp.zeros(v_ref.shape[1:], jnp.bfloat16)
+    attend(req_ref, q_ref, k_ref, v_ref, BLOCKS // 2, out_refs, score_ref)
+
+
+def attend_near_kernel(req_ref, q_ref, k_ref, v_ref, *refs):
+    attend(req_ref, q_ref, k_ref, v_ref, 0, refs[:LINES], refs[LINES])
+
+
+def finish_kernel(moved_ref, lo_ref, hi_ref, *refs):
+    in_refs, out_ref = refs[:BLOCKS], refs[BLOCKS]
+    line = lax.axis_index("sp")
+    wide = in_refs[0].shape[2]
+    cols = wide // 2
+    low = iota((1, wide), 1) < cols
+    for pair in range(LINES // 2):
+        lo, hi = [], []
+        for k in (2 * pair, 2 * pair + 1):
+            rows = jnp.concatenate([ref[line ^ k] for ref in in_refs], axis=0)
+            lo.append(dot_n(lo_ref[...], rows))
+            hi.append(dot_n(hi_ref[...], rows))
+        back = jnp.where(low, lo[0], hi[1]) + pltpu.roll(jnp.where(low, lo[1], hi[0]), cols, 1)
+        span = slice(pair * wide, (pair + 1) * wide)
+        out_ref[:, span] = (moved_ref[:, span].astype(jnp.float32) + back).astype(jnp.bfloat16)
+
+
+def smem():
+    return pl.BlockSpec(memory_space=pltpu.SMEM)
+
+
+def vmem():
+    return pl.BlockSpec(memory_space=pltpu.VMEM)
+
+
+def room(mib):
+    return pltpu.CompilerParams(vmem_limit_bytes=mib << 20)
+
+
+def kept(shape, dtype=jnp.bfloat16):
+    return jax.ShapeDtypeStruct(shape, dtype)
+
+
+def to_block(x, b):
+    j, r = b // SEC, b % SEC
+    pairs = [
+        (s * PLANES + d, (s ^ r) * PLANES + (d ^ j)) for s in range(SEC) for d in range(PLANES)
+    ]
+    return lax.ppermute(x, ("sec", "dev"), pairs)
+
+
+def to_line(x, m):
+    return lax.ppermute(x, "sp", [(i, i ^ m) for i in range(LINES)])
+
+
+def spread(came, planes):
+    a = jnp.stack([came[SEC * j] for j in planes])[None]
+    b = jnp.stack([came[SEC * j + 1] for j in planes])[None]
+    a2 = jnp.concatenate([a, to_line(a, 1)], axis=0)
+    b2 = jnp.concatenate([b, to_line(b, 2)], axis=0)
+    return [a2, to_line(a2, 2), b2, to_line(b2, 1)]
+
+
+def shards(*args):
+    return shards_here(*args)
+
+
+def shards_here(
+    patch_qkv, patch_state, window_index, patch_owner, source_request, norm_gain, w_qkv, b_qkv
+):
+    rows, _, width = patch_qkv.shape
+    cap = 2 * rows // BLOCKS
+    cols = w_qkv.shape[2]
+    half = cap // 2
+    block_rows = LINES * cap
+    heads = cols // HD
+
+    moved, lo, hi, *sent = pl.pallas_call(
+        window_kernel,
+        out_shape=[kept((rows, width)), kept((rows, rows)), kept((rows, rows))]
+        + [kept((cap, width))] * BLOCKS,
+        in_specs=[pl.BlockSpec(memory_space=pltpu.HBM)] * 2 + [vmem()] * 2,
+        out_specs=[vmem()] * (3 + BLOCKS),
+        scratch_shapes=[
+            pltpu.VMEM((3, rows, width), jnp.bfloat16),
+            pltpu.VMEM((rows, width), jnp.bfloat16),
+            pltpu.VMEM((width, rows), jnp.bfloat16),
+            pltpu.VMEM((width, rows), jnp.bfloat16),
+            pltpu.VMEM((width // HD, rows, rows), jnp.float32),
+            pltpu.VMEM((BLOCKS * cap, rows), jnp.bfloat16),
+            pltpu.VMEM((BLOCKS * cap, LANES), jnp.float32),
+            pltpu.SemaphoreType.DMA((5,)),
+        ],
+        name="window",
+        compiler_params=room(WINDOW_MIB),
+    )(jnp.transpose(patch_qkv, (1, 0, 2)), patch_state, window_index, patch_owner.reshape(1, rows))
+
+    came = [sent[0] if b == 0 else to_block(sent[b], b) for b in range(BLOCKS)]
+    gathered = [spread(came, planes) for planes in GROUPS]
+
+    key_bias = b_qkv[1].astype(jnp.float32).reshape(heads, HD)
+    gain = norm_gain.reshape(1, width)
+    shared = (gain, jnp.transpose(w_qkv, (1, 2, 0)), b_qkv, key_bias)
+
+    def projected(pieces, planes):
+        return pl.pallas_call(
+            project_kernel,
+            out_shape=[kept(shape) for shape in stores(SEC * planes, block_rows, cols)],
+            in_specs=[vmem()] * 8,
+            out_specs=[vmem()] * 3,
+            scratch_shapes=[pltpu.VMEM((SEC * block_rows, width), jnp.bfloat16)],
+            name="project",
+            compiler_params=room(16),
+            cost_estimate=pl.CostEstimate(
+                flops=2 * SEC * planes * block_rows * width * 4 * cols, bytes_accessed=4 << 20, transcendentals=0
+            ),
+        )(*pieces, *shared)
+
+    ready = []
+    for i, planes in enumerate(GROUPS[:-1]):
+        ready += projected(gathered[i], len(planes))
+    q_store = stores(BLOCKS, block_rows, cols)[0]
+    _, k_store, v_store = stores(BLOCKS + 1, block_rows, cols)
+    scores = pltpu.VMEM((heads, BLOCKS // 2 * block_rows, block_rows), jnp.float32)
+    *far_mixed, queries, keys, values = pl.pallas_call(
+        functools.partial(attend_far_kernel, GROUPS),
+        out_shape=[kept((BLOCKS // 2, half, 2 * cols))] * LINES + [kept(q_store), kept(k_store), kept(v_store)],
+        in_specs=[smem()] + [vmem()] * (len(ready) + 8),
+        out_specs=[vmem()] * (LINES + 3),
+        scratch_shapes=[pltpu.VMEM((SEC * block_rows, width), jnp.bfloat16), scores],
+        name="attend_far",
+        compiler_params=room(20),
+    )(source_request, *ready, *gathered[-1], *shared)
+    near_mixed = pl.pallas_call(
+        attend_near_kernel,
+        out_shape=[kept((BLOCKS // 2, half, 2 * cols))] * LINES,
+        in_specs=[smem()] + [vmem()] * 3,
+        out_specs=[vmem()] * LINES,
+        scratch_shapes=[scores],
+        name="attend_near",
+        compiler_params=room(12),
+        cost_estimate=pl.CostEstimate(flops=4 << 30, bytes_accessed=6 << 20, transcendentals=2 << 20),
+    )(source_request, queries, keys, values)
+
+    far_lines = [far_mixed[0]] + [to_line(far_mixed[m], m) for m in range(1, LINES)]
+    near_lines = [near_mixed[0]] + [to_line(near_mixed[m], m) for m in range(1, LINES)]
+    back = []
+    for b in range(BLOCKS):
+        lines, at = (far_lines, b - BLOCKS // 2) if b >= BLOCKS // 2 else (near_lines, b)
+        joined = jnp.stack([line[at] for line in lines])
+        back.append(joined if b == 0 else to_block(joined, b))
+
+    return pl.pallas_call(
+        finish_kernel,
+        out_shape=kept((rows, width)),
+        in_specs=[vmem()] * (3 + BLOCKS),
+        out_specs=vmem(),
+        name="finish",
+        compiler_params=room(8),
+    )(moved, lo, hi, *back)
+
+
 def solution(mesh):
     in_specs = (
         P(("sec", "sp", "dev"), None, None),
@@ -126,4 +550,7 @@
         P(None, "sp"),
     )
     out_specs = P(("sec", "sp", "dev"), None)
-    return jax.shard_map(shards, mesh=mesh, in_specs=in_specs, out_specs=out_specs, check_vma=False)
+    sizes = (mesh.shape["sec"], mesh.shape["sp"], mesh.shape["dev"])
+    special = sizes == (SEC, LINES, PLANES)
+    body = shards if special else shards_general
+    return jax.shard_map(body, mesh=mesh, in_specs=in_specs, out_specs=out_specs, check_vma=False)

time: 186 us -> 90.5 us (0.49)
  blocking collectives: 69.4 us -> 0 us
  matrix products: 38.1 us -> 0 us
  starting transfers between devices: 3.26 us -> 39 us
  local copies, waits for them, and re-layouts: 23.6 us -> 0.89 us
  Pallas kernels: 0 us -> 18.9 us
  between operations: 13.6 us -> 0.36 us
  other arithmetic: 7.76 us -> 1.89 us
  loops' own time: 4.17 us -> 0 us
  waiting for transfers between devices: 25.6 us -> 27.9 us
    all_to_all x3 -> x0, blocking collectives: 60.6 us -> none  [the longest x1 24.2 us: shards(): lax.all_to_all(outgoing, ('sec', 'dev'), split_axis=0, concat_axis=0, til...]
    ppermute x0 -> x32, starting transfers between devices: none -> 39 us  [the longest x18 21.1 us: to_line(): return lax.ppermute(x, 'sp', [(i, i ^ m) for i in range(LINES)])]
    ppermute x0 -> x32, waiting for transfers between devices: none -> 27.9 us  [the longest x18 14.6 us: to_line(): return lax.ppermute(x, 'sp', [(i, i ^ m) for i in range(LINES)])]
    dot_general x7 -> x0, matrix products: 20.9 us -> none  [the longest x2 11.4 us: one_block(): jnp.einsum('hqk,khd->qhd', weights, values_all, preferred_element_type=jn...]
    all_gather x1 -> x0, waiting for transfers between devices: 20.2 us -> none  [shards(): lax.all_gather(incoming, 'sp', axis=1, tiled=True)]
    pallas_call x0 -> x6, Pallas kernels: none -> 18.9 us  [the longest x1 5.34 us: shards_here(): pl.pallas_call(functools.partial(attend_far_kernel, GROUPS), out_shape=[k...]
    sub x3 -> x0, matrix products: 17.2 us -> none  [softmax_rows(): expo_vals = jnp.exp(scores - row_max)]
    all_gather x1 -> x0, blocking collectives: 8.73 us -> none  [shards(): lax.all_gather(arrived, 'sp', axis=1, tiled=True)]
  transfers between devices with their start and end apart: 2 -> 32, of which waited for: 2 -> 10; matrix products, arithmetic and copies ran while one was open for 0% -> 3% of each run, Pallas kernels for 0% -> 5%
where the time goes in v1:
time: 90.5 us; the launch traced here: 88.9 us
  starting transfers between devices  39 us (43%)
  waiting for transfers between devices  27.9 us (31%)
  Pallas kernels  18.9 us (21%)
  other arithmetic  1.89 us (2%)
    ppermute x18, starting transfers between devices, to_line(): return lax.ppermute(x, 'sp', [(i, i ^ m) for i in range(LINES)])  21.1 us
    ppermute x14, starting transfers between devices, to_block(): return lax.ppermute(x, ('sec', 'dev'), pairs)  17.9 us
    ppermute x18, waiting for transfers between devices, to_line(): return lax.ppermute(x, 'sp', [(i, i ^ m) for i in range(LINES)])  14.6 us
    ppermute x14, waiting for transfers between devices, to_block(): return lax.ppermute(x, ('sec', 'dev'), pairs)  13.3 us
    pallas_call x1, Pallas kernels, shards_here(): pl.pallas_call(functools.partial(attend_far_kernel, GROUPS), out_shape=[k...  5.34 us
    pallas_call x1, Pallas kernels, shards_here(): pl.pallas_call(window_kernel, out_shape=[kept((rows, width)), kept((rows,...  4.31 us
    pallas_call x2, Pallas kernels, projected(): pl.pallas_call(project_kernel, out_shape=[kept(shape) for shape in stores...  4.1 us
    pallas_call x1, Pallas kernels, shards_here(): pl.pallas_call(attend_near_kernel, out_shape=[kept((BLOCKS // 2, half, 2...  3.81 us
  transfers between devices with their start and end apart: 32, of which 10 were waited for; matrix products, arithmetic and copies ran while one was open for 3% of the time, Pallas kernels for 5%

profile of v1, /device:TPU:0, one launch (start us, length us, event | category | flops | bytes accessed | tf_op | source)
XLA Modules:
  0.0 88.9 jit_solution(11312237746038798372)
XLA Ops:
  0.0 4.3 %window.1 = (bf16[128,1280]{1,0:T(8,128)(2,1)}, bf16[128,128]{1,0:T(8,128)(2,1)}, bf16[128,128]{1,0:T(8,128)(2,1)}, bf16[32,1280]{1,0:T(8,128)(2,1)}, bf16[32,12...) custom-call(bf16[3,128,1280]{2,1,0:T(8,128)(2,1)} %bitcast.18, ...), custom_call_target="tpu_custom_call" | custom-call | tf_op jit(solution)/shard_map/window/pallas_call | solution.py:456
  4.3 0.6 collective-permute-start.2
  4.9 2.6 %collective-permute-start.5 = (bf16[32,1280]{1,0:T(8,128)(2,1)}, bf16[32,1280]{1,0:T(8,128)(2,1)S(1)}, u32[]{:S(2)}, u32[]{:S(2)}) collective-permute-start(bf16[32,1280]{1,0:T(8,128)(2,1)} %get-tuple-element.41), channel_id=1, source_target_pairs={{0,1},{1,0},{2,3},{3,2},{16,17},{17,16},{18,19},{19,18},{4,5},{5,4... | collective-permute-start | bytes 245768 | tf_op jit(solution)/shard_map/ppermute | solution.py:427
  7.5 2.6 %collective-permute-start.6 = (bf16[32,1280]{1,0:T(8,128)(2,1)}, bf16[32,1280]{1,0:T(8,128)(2,1)S(1)}, u32[]{:S(2)}, u32[]{:S(2)}) collective-permute-start(bf16[32,1280]{1,0:T(8,128)(2,1)} %get-tuple-element.42), channel_id=1, source_target_pairs={{0,2},{1,3},{2,0},{3,1},{16,18},{17,19},{18,16},{19,17},{4,6},{5,7... | collective-permute-start | bytes 245768 | tf_op jit(solution)/shard_map/ppermute | solution.py:427
  10.1 0.2 collective-permute-start.10
  10.3 0.7 convert_reduce_fusion
  11.0 0.1 reshape.12.refs_7_.refs_13_
  11.1 0.7 reshape.11.refs_4_.refs_10_
  11.8 5.0 %collective-permute-done.9 = bf16[32,1280]{1,0:T(8,128)(2,1)S(1)} collective-permute-done((bf16[32,1280]{1,0:T(8,128)(2,1)}, bf16[32,1280]{1,0:T(8,128)(2,1)S(1)}, u32[]{:S(2)}, u32[]{:S(2)}) %collective-permute-start.9) | collective-permute-done | bytes 81952 | tf_op jit(solution)/shard_map/ppermute | solution.py:427
  16.8 0.8 collective-permute-start.13
  17.6 0.0 collective-permute-done.10
  17.6 2.8 %collective-permute-start.16 = (bf16[32,1280]{1,0:T(8,128)(2,1)}, bf16[32,1280]{1,0:T(8,128)(2,1)S(1)}, u32[]{:S(2)}, u32[]{:S(2)}) collective-permute-start(bf16[32,1280]{1,0:T(8,128)(2,1)} %get-tuple-element.49), channel_id=1, source_target_pairs={{0,19},{1,18},{2,17},{3,16},{16,3},{17,2},{18,1},{19,0},{4,23},{5,... | collective-permute-start | bytes 245768 | tf_op jit(solution)/shard_map/ppermute | solution.py:427
  20.4 0.0 collective-permute-done.2
  20.4 1.6 %collective-permute-start = (bf16[1,1,32,1280]{3,2,1,0:T(8,128)(2,1)}, bf16[1,1,32,1280]{3,2,1,0:T(8,128)(2,1)S(1)}, u32[]{:S(2)}, u32[]{:S(2)}) collective-permute-start(bf16[1,1,32,1280]{3,2,1,0:T(8,128)(2,1)} %bitcast.23), channel_id=1, source_target_pairs={{0,4},{4,0},{8,12},{12,8},{1,5},{5,1},{9,13},{13,9},{2,6},{6,2},{1... | collective-permute-start | bytes 245768 | tf_op jit(solution)/shard_map/ppermute | solution.py:431
  21.9 0.0 collective-permute-done.5
  21.9 1.5 %collective-permute-start.3 = (bf16[1,1,32,1280]{3,2,1,0:T(8,128)(2,1)S(1)}, bf16[1,1,32,1280]{3,2,1,0:T(8,128)(2,1)S(1)}, u32[]{:S(2)}, u32[]{:S(2)}) collective-permute-start(bf16[1,1,32,1280]{3,2,1,0:T(8,128)(2,1)S(1)} %bitcast.19), channel_id=1, source_target_pairs={{0,8},{4,12},{8,0},{12,4},{1,9},{5,13},{9,1},{13,5},{2,10},{6,14},... | collective-permute-start | bytes 245768 | tf_op jit(solution)/shard_map/ppermute | solution.py:431
  23.5 0.7 collective-permute-done.13
  24.2 1.5 %collective-permute-start.14 = (bf16[1,1,32,1280]{3,2,1,0:T(8,128)(2,1)S(1)}, bf16[1,1,32,1280]{3,2,1,0:T(8,128)(2,1)S(1)}, u32[]{:S(2)}, u32[]{:S(2)}) collective-permute-start(bf16[1,1,32,1280]{3,2,1,0:T(8,128)(2,1)S(1)} %bitcast.21), channel_id=1, source_target_pairs={{0,4},{4,0},{8,12},{12,8},{1,5},{5,1},{9,13},{13,9},{2,6},{6,2},{1... | collective-permute-start | bytes 245768 | tf_op jit(solution)/shard_map/ppermute | solution.py:431
  25.7 0.0 collective-permute-done.16
  25.7 1.5 %collective-permute-start.17 = (bf16[1,1,32,1280]{3,2,1,0:T(8,128)(2,1)S(1)}, bf16[1,1,32,1280]{3,2,1,0:T(8,128)(2,1)S(1)}, u32[]{:S(2)}, u32[]{:S(2)}) collective-permute-start(bf16[1,1,32,1280]{3,2,1,0:T(8,128)(2,1)S(1)} %bitcast.27), channel_id=1, source_target_pairs={{0,8},{4,12},{8,0},{12,4},{1,9},{5,13},{9,1},{13,5},{2,10},{6,14},... | collective-permute-start | bytes 245768 | tf_op jit(solution)/shard_map/ppermute | solution.py:431
  27.2 0.0 collective-permute-done.6
  27.2 0.5 collective-permute-start.11
  27.7 0.6 collective-permute-start.7
  28.3 0.9 %pad_maximum_fusion.2.refs_0_ = bf16[2,1,32,1280]{3,2,1,0:T(8,128)(2,1)S(1)} fusion(bf16[1,1,32,1280]{3,2,1,0:T(8,128)(2,1)S(1)} %collective-permute-done, bf16[1,1,32,1280]{3,2,1,0:T(8,128)(2,1)} %bitcast.24), kind=kLoop, calls=%fused_computation.2 | loop fusion | flops 81920 | bytes 327680 | tf_op jit(solution)/shard_map/concatenate | solution.py:437
  29.2 1.8 %collective-permute-done.17 = bf16[1,1,32,1280]{3,2,1,0:T(8,128)(2,1)S(1)} collective-permute-done((bf16[1,1,32,1280]{3,2,1,0:T(8,128)(2,1)S(1)}, bf16[1,1,32,1280]{3,2,1,0:T(8,128)(2,1)S(1)}, u32[]{:S(2)}, u32[]{:S(2)}) %collective-permute-start.17) | collective-permute-done | bytes 81952 | tf_op jit(solution)/shard_map/ppermute | solution.py:431
  31.0 1.5 %collective-permute-start.1 = (bf16[2,1,32,1280]{3,2,1,0:T(8,128)(2,1)S(1)}, bf16[2,1,32,1280]{3,2,1,0:T(8,128)(2,1)S(1)}, u32[]{:S(2)}, u32[]{:S(2)}) collective-permute-start(bf16[2,1,32,1280]{3,2,1,0:T(8,128)(2,1)S(1)} %pad_maximum_fusion.2.refs_0_), channel_id=1, source_target_pairs={{0,8},{4,12},{8,0},{12,4},{1,9},{5,13},{9,1},{13,5},{2,10},{6,14},... | collective-permute-start | bytes 491528 | tf_op jit(solution)/shard_map/ppermute | solution.py:431
  32.5 0.6 collective-permute-done.7
  33.1 1.0 %collective-permute-start.18 = (bf16[2,1,32,1280]{3,2,1,0:T(8,128)(2,1)S(1)}, bf16[2,1,32,1280]{3,2,1,0:T(8,128)(2,1)S(1)}, u32[]{:S(2)}, u32[]{:S(2)}) collective-permute-start(bf16[2,1,32,1280]{3,2,1,0:T(8,128)(2,1)S(1)} %pad_maximum_fusion.5.refs_8_), channel_id=1, source_target_pairs={{0,4},{4,0},{8,12},{12,8},{1,5},{5,1},{9,13},{13,9},{2,6},{6,2},{1... | collective-permute-start | bytes 491528 | tf_op jit(solution)/shard_map/ppermute | solution.py:431
  34.2 0.3 collective-permute-done.11
  34.5 1.4 %collective-permute-start.8 = (bf16[2,2,32,1280]{3,2,1,0:T(8,128)(2,1)S(1)}, bf16[2,2,32,1280]{3,2,1,0:T(8,128)(2,1)S(1)}, u32[]{:S(2)}, u32[]{:S(2)}) collective-permute-start(bf16[2,2,32,1280]{3,2,1,0:T(8,128)(2,1)S(1)} %pad_maximum_fusion.refs_0_), channel_id=1, source_target_pairs={{0,8},{4,12},{8,0},{12,4},{1,9},{5,13},{9,1},{13,5},{2,10},{6,14},... | collective-permute-start | bytes 983048 | tf_op jit(solution)/shard_map/ppermute | solution.py:431
  35.9 0.0 collective-permute-done.3
  35.9 1.0 %collective-permute-start.12 = (bf16[2,2,32,1280]{3,2,1,0:T(8,128)(2,1)S(1)}, bf16[2,2,32,1280]{3,2,1,0:T(8,128)(2,1)S(1)}, u32[]{:S(2)}, u32[]{:S(2)}) collective-permute-start(bf16[2,2,32,1280]{3,2,1,0:T(8,128)(2,1)S(1)} %pad_maximum_fusion.1.refs_2_), channel_id=1, source_target_pairs={{0,4},{4,0},{8,12},{12,8},{1,5},{5,1},{9,13},{13,9},{2,6},{6,2},{1... | collective-permute-start | bytes 983048 | tf_op jit(solution)/shard_map/ppermute | solution.py:431
  36.9 0.0 collective-permute-done.14
  36.9 1.2 %collective-permute-start.4 = (bf16[2,1,32,1280]{3,2,1,0:T(8,128)(2,1)S(1)}, bf16[2,1,32,1280]{3,2,1,0:T(8,128)(2,1)S(1)}, u32[]{:S(2)}, u32[]{:S(2)}) collective-permute-start(bf16[2,1,32,1280]{3,2,1,0:T(8,128)(2,1)S(1)} %pad_maximum_fusion.3.refs_2_), channel_id=1, source_target_pairs={{0,4},{4,0},{8,12},{12,8},{1,5},{5,1},{9,13},{13,9},{2,6},{6,2},{1... | collective-permute-start | bytes 491528 | tf_op jit(solution)/shard_map/ppermute | solution.py:431
  38.1 0.7 collective-permute-start.15
  38.8 10.1 %collective-permute-done.4.refs_3_ = bf16[2,1,32,1280]{3,2,1,0:T(8,128)(2,1)S(1)} collective-permute-done((bf16[2,1,32,1280]{3,2,1,0:T(8,128)(2,1)S(1)}, bf16[2,1,32,1280]{3,2,1,0:T(8,128)(2,1)S(1)}, u32[]{:S(2)}, u32[]{:S(2)}) %collective-permute-start.4) | collective-permute-done | bytes 163872 | tf_op jit(solution)/shard_map/ppermute | solution.py:431
  49.0 1.5 %project.2 = (bf16[2,4,128,128]{3,2,1,0:T(8,128)(2,1)S(1)}, bf16[2,128,512]{2,1,0:T(8,128)(2,1)S(1)}, bf16[2,320,128]{2,1,0:T(8,128)(2,1)S(1)}) custom-call(bf16[2,1,32,1280]{3,2,1,0:T(8,128)(2,1)S(1)} %pad_maximum_fusion.2.refs_0_, bf16[2,1,32,1280]{3,2,1,0:T(8,128)(2,1)S(1)} %collective-permute-done.1.refs_1_, ...), custom_call_target="tpu_custom_call" | custom-call | flops 838860800 | bytes 4194304 | tf_op jit(solution)/shard_map/project/pallas_call | solution.py:484
  50.5 0.0 copy-start.5
  50.5 0.0 collective-permute-done.8.refs_1_
  50.5 0.0 collective-permute-done.12.refs_3_
  50.5 2.6 %project.3 = (bf16[4,4,128,128]{3,2,1,0:T(8,128)(2,1)S(1)}, bf16[4,128,512]{2,1,0:T(8,128)(2,1)S(1)}, bf16[4,320,128]{2,1,0:T(8,128)(2,1)S(1)}) custom-call(bf16[2,2,32,1280]{3,2,1,0:T(8,128)(2,1)S(1)} %pad_maximum_fusion.refs_0_, bf16[2,2,32,1280]{3,2,1,0:T(8,128)(2,1)S(1)} %collective-permute-done.8.refs_1_, ...), custom_call_target="tpu_custom_call" | custom-call | flops 1677721600 | bytes 4194304 | tf_op jit(solution)/shard_map/project/pallas_call | solution.py:484
  53.1 0.0 collective-permute-done.18.refs_9_
  53.1 5.3 %attend_far.1 = (bf16[4,16,640]{2,1,0:T(8,128)(2,1)S(1)}, bf16[4,16,640]{2,1,0:T(8,128)(2,1)S(1)}, bf16[4,16,640]{2,1,0:T(8,128)(2,1)S(1)}, bf16[4,16,640]{2,1,0...) custom-call(s32[1,8]{1,0:T(1,128)S(1)} %copy-done.5, ...), custom_call_target="tpu_custom_call" | custom-call | tf_op jit(solution)/shard_map/attend_far/pallas_call | solution.py:503
  58.5 3.8 %attend_near.1 = (bf16[4,16,640]{2,1,0:T(8,128)(2,1)S(1)}, bf16[4,16,640]{2,1,0:T(8,128)(2,1)S(1)}, bf16[4,16,640]{2,1,0:T(8,128)(2,1)S(1)}, bf16[4,16,640]{2,1,0:T(8,128)(2,1)S(1)}) custom-call(s32[1,8]{1,0:T(1,128)S(1)} %copy-done.5, bf16[8,4,128,128]{3,2,1,0:T(8,128)(2,1)S(1)} %get-tuple-element.50.q_ref, ...), custom_call_target="tpu_custom_call" | custom-call | flops 4294967296 | bytes 6291456 | tf_op jit(solution)/shard_map/attend_near/pallas_call | solution.py:512
  62.3 0.0 copy-start.1
  62.4 1.1 %collective-permute-start.19 = (bf16[4,16,640]{2,1,0:T(8,128)(2,1)S(1)}, bf16[4,16,640]{2,1,0:T(8,128)(2,1)S(1)}, u32[]{:S(2)}, u32[]{:S(2)}) collective-permute-start(bf16[4,16,640]{2,1,0:T(8,128)(2,1)S(1)} %get-tuple-element.54), channel_id=1, source_target_pairs={{0,4},{4,0},{8,12},{12,8},{1,5},{5,1},{9,13},{13,9},{2,6},{6,2},{1... | collective-permute-start | bytes 245768 | tf_op jit(solution)/shard_map/ppermute | solution.py:431
  63.5 1.2 %collective-permute-start.20 = (bf16[4,16,640]{2,1,0:T(8,128)(2,1)S(1)}, bf16[4,16,640]{2,1,0:T(8,128)(2,1)S(1)}, u32[]{:S(2)}, u32[]{:S(2)}) collective-permute-start(bf16[4,16,640]{2,1,0:T(8,128)(2,1)S(1)} %get-tuple-element.55), channel_id=1, source_target_pairs={{0,8},{4,12},{8,0},{12,4},{1,9},{5,13},{9,1},{13,5},{2,10},{6,14},... | collective-permute-start | bytes 245768 | tf_op jit(solution)/shard_map/ppermute | solution.py:431
  64.7 1.3 %collective-permute-start.21 = (bf16[4,16,640]{2,1,0:T(8,128)(2,1)S(1)}, bf16[4,16,640]{2,1,0:T(8,128)(2,1)S(1)}, u32[]{:S(2)}, u32[]{:S(2)}) collective-permute-start(bf16[4,16,640]{2,1,0:T(8,128)(2,1)S(1)} %get-tuple-element.56), channel_id=1, source_target_pairs={{0,12},{4,8},{8,4},{12,0},{1,13},{5,9},{9,5},{13,1},{2,14},{6,10},... | collective-permute-start | bytes 245768 | tf_op jit(solution)/shard_map/ppermute | solution.py:431
  66.0 1.0 %collective-permute-start.25 = (bf16[4,16,640]{2,1,0:T(8,128)(2,1)S(1)}, bf16[4,16,640]{2,1,0:T(8,128)(2,1)S(1)}, u32[]{:S(2)}, u32[]{:S(2)}) collective-permute-start(bf16[4,16,640]{2,1,0:T(8,128)(2,1)S(1)} %get-tuple-element.58), channel_id=1, source_target_pairs={{0,4},{4,0},{8,12},{12,8},{1,5},{5,1},{9,13},{13,9},{2,6},{6,2},{1... | collective-permute-start | bytes 245768 | tf_op jit(solution)/shard_map/ppermute | solution.py:431
  67.0 1.2 %collective-permute-start.26 = (bf16[4,16,640]{2,1,0:T(8,128)(2,1)S(1)}, bf16[4,16,640]{2,1,0:T(8,128)(2,1)S(1)}, u32[]{:S(2)}, u32[]{:S(2)}) collective-permute-start(bf16[4,16,640]{2,1,0:T(8,128)(2,1)S(1)} %get-tuple-element.59), channel_id=1, source_target_pairs={{0,8},{4,12},{8,0},{12,4},{1,9},{5,13},{9,1},{13,5},{2,10},{6,14},... | collective-permute-start | bytes 245768 | tf_op jit(solution)/shard_map/ppermute | solution.py:431
  68.2 0.0 collective-permute-done.19
  68.2 1.3 %collective-permute-start.27 = (bf16[4,16,640]{2,1,0:T(8,128)(2,1)S(1)}, bf16[4,16,640]{2,1,0:T(8,128)(2,1)S(1)}, u32[]{:S(2)}, u32[]{:S(2)}) collective-permute-start(bf16[4,16,640]{2,1,0:T(8,128)(2,1)S(1)} %get-tuple-element.60), channel_id=1, source_target_pairs={{0,12},{4,8},{8,4},{12,0},{1,13},{5,9},{9,5},{13,1},{2,14},{6,10},... | collective-permute-start | bytes 245768 | tf_op jit(solution)/shard_map/ppermute | solution.py:431
  69.5 0.9 %collective-permute-done.20 = bf16[4,16,640]{2,1,0:T(8,128)(2,1)S(1)} collective-permute-done((bf16[4,16,640]{2,1,0:T(8,128)(2,1)S(1)}, bf16[4,16,640]{2,1,0:T(8,128)(2,1)S(1)}, u32[]{:S(2)}, u32[]{:S(2)}) %collective-permute-start.20) | collective-permute-done | bytes 81952 | tf_op jit(solution)/shard_map/ppermute | solution.py:431
  70.5 0.1 collective-permute-start.22
  70.6 1.7 %collective-permute-start.23 = (bf16[4,16,640]{2,1,0:T(8,128)(2,1)S(1)}, bf16[4,16,640]{2,1,0:T(8,128)(2,1)S(1)}, u32[]{:S(2)}, u32[]{:S(2)}) collective-permute-start(bf16[4,16,640]{2,1,0:T(8,128)(2,1)S(1)} %pad_maximum_fusion.8), channel_id=1, source_target_pairs={{0,1},{1,0},{2,3},{3,2},{16,17},{17,16},{18,19},{19,18},{4,5},{5,4... | collective-permute-start | bytes 245768 | tf_op jit(solution)/shard_map/ppermute | solution.py:427
  72.3 0.3 collective-permute-start.24
  72.6 0.9 collective-permute-done.27
  73.6 2.4 %collective-permute-start.28 = (bf16[4,16,640]{2,1,0:T(8,128)(2,1)S(1)}, bf16[4,16,640]{2,1,0:T(8,128)(2,1)S(1)}, u32[]{:S(2)}, u32[]{:S(2)}) collective-permute-start(bf16[4,16,640]{2,1,0:T(8,128)(2,1)S(1)} %pad_maximum_fusion.10), channel_id=1, source_target_pairs={{0,2},{1,3},{2,0},{3,1},{16,18},{17,19},{18,16},{19,17},{4,6},{5,7... | collective-permute-start | bytes 245768 | tf_op jit(solution)/shard_map/ppermute | solution.py:427
  76.0 0.1 collective-permute-start.29
  76.1 2.0 %collective-permute-start.30 = (bf16[4,16,640]{2,1,0:T(8,128)(2,1)S(1)}, bf16[4,16,640]{2,1,0:T(8,128)(2,1)S(1)}, u32[]{:S(2)}, u32[]{:S(2)}) collective-permute-start(bf16[4,16,640]{2,1,0:T(8,128)(2,1)S(1)} %pad_maximum_fusion.12), channel_id=1, source_target_pairs={{0,3},{1,2},{2,1},{3,0},{16,19},{17,18},{18,17},{19,16},{4,7},{5,6... | collective-permute-start | bytes 245768 | tf_op jit(solution)/shard_map/ppermute | solution.py:427
  78.1 1.9 %collective-permute-start.31 = (bf16[4,16,640]{2,1,0:T(8,128)(2,1)S(1)}, bf16[4,16,640]{2,1,0:T(8,128)(2,1)S(1)}, u32[]{:S(2)}, u32[]{:S(2)}) collective-permute-start(bf16[4,16,640]{2,1,0:T(8,128)(2,1)S(1)} %pad_maximum_fusion.13), channel_id=1, source_target_pairs={{0,19},{1,18},{2,17},{3,16},{16,3},{17,2},{18,1},{19,0},{4,23},{5,... | collective-permute-start | bytes 245768 | tf_op jit(solution)/shard_map/ppermute | solution.py:427
  80.1 6.1 %collective-permute-done.28.refs_4_ = bf16[4,16,640]{2,1,0:T(8,128)(2,1)S(1)} collective-permute-done((bf16[4,16,640]{2,1,0:T(8,128)(2,1)S(1)}, bf16[4,16,640]{2,1,0:T(8,128)(2,1)S(1)}, u32[]{:S(2)}, u32[]{:S(2)}) %collective-permute-start.28) | collective-permute-done | bytes 81952 | tf_op jit(solution)/shard_map/ppermute | solution.py:427
  86.1 1.5 %collective-permute-done.29.refs_5_ = bf16[4,16,640]{2,1,0:T(8,128)(2,1)S(1)} collective-permute-done((bf16[4,16,640]{2,1,0:T(8,128)(2,1)S(1)}, bf16[4,16,640]{2,1,0:T(8,128)(2,1)S(1)}, u32[]{:S(2)}, u32[]{:S(2)}) %collective-permute-start.29) | collective-permute-done | bytes 81952 | tf_op jit(solution)/shard_map/ppermute | solution.py:427
  87.7 1.3 %finish.1 = bf16[128,1280]{1,0:T(8,128)(2,1)} custom-call(bf16[128,1280]{1,0:T(8,128)(2,1)S(1)} %copy-done.1, bf16[128,128]{1,0:T(8,128)(2,1)S(1)} %copy-done.2, bf16[128,128]{1,0:T(8,128)(2,1)S(1)} %copy-done.3, bf16[4,16,640]{2,1,0:T(8,128)(2,1)S(1)} %pad_maximum_fusion.6.refs_0_, bf16[4,16,640]{2,1,0:T(8,128)(2,1)S(1)} %collective-permute-done.22.refs_1_, ...), custom_call_target="tpu_custom_call" | custom-call | tf_op jit(solution)/shard_map/finish/pallas_call | solution.py:531
  (45 shorter events, 0.4 us)
Async XLA Ops:
  0.0 49.0 %copy-start.4 = (bf16[3,320]{1,0:T(4,128)(2,1)S(1)}, bf16[3,320]{1,0:T(4,128)(2,1)}, u32[]{:S(2)}) copy-start(bf16[3,320]{1,0:T(4,128)(2,1)} %refs_12_.1) | copy-start | bytes 5764
  0.0 49.0 %copy-start = (bf16[1280,3,320]{0,2,1:T(8,128)(2,1)S(1)}, bf16[1280,3,320]{0,2,1:T(8,128)(2,1)}, u32[]{:S(2)}) copy-start(bf16[1280,3,320]{0,2,1:T(8,128)(2,1)} %param.14) | copy-start | bytes 7372804
  4.3 16.0 %collective-permute-start.2 = (bf16[32,1280]{1,0:T(8,128)(2,1)}, bf16[32,1280]{1,0:T(8,128)(2,1)S(1)}, u32[]{:S(2)}, u32[]{:S(2)}) collective-permute-start(bf16[32,1280]{1,0:T(8,128)(2,1)} %get-tuple-element.37), channel_id=1, source_target_pairs={{0,16},{1,17},{2,18},{3,19},{16,0},{17,1},{18,2},{19,3},{4,20},{5,... | collective-permute-start | bytes 245768 | tf_op jit(solution)/shard_map/ppermute | solution.py:427
  4.9 17.1 %collective-permute-start.5 = (bf16[32,1280]{1,0:T(8,128)(2,1)}, bf16[32,1280]{1,0:T(8,128)(2,1)S(1)}, u32[]{:S(2)}, u32[]{:S(2)}) collective-permute-start(bf16[32,1280]{1,0:T(8,128)(2,1)} %get-tuple-element.41), channel_id=1, source_target_pairs={{0,1},{1,0},{2,3},{3,2},{16,17},{17,16},{18,19},{19,18},{4,5},{5,4... | collective-permute-start | bytes 245768 | tf_op jit(solution)/shard_map/ppermute | solution.py:427
  7.5 19.7 %collective-permute-start.6 = (bf16[32,1280]{1,0:T(8,128)(2,1)}, bf16[32,1280]{1,0:T(8,128)(2,1)S(1)}, u32[]{:S(2)}, u32[]{:S(2)}) collective-permute-start(bf16[32,1280]{1,0:T(8,128)(2,1)} %get-tuple-element.42), channel_id=1, source_target_pairs={{0,2},{1,3},{2,0},{3,1},{16,18},{17,19},{18,16},{19,17},{4,6},{5,7... | collective-permute-start | bytes 245768 | tf_op jit(solution)/shard_map/ppermute | solution.py:427
  10.1 6.7 %collective-permute-start.9 = (bf16[32,1280]{1,0:T(8,128)(2,1)}, bf16[32,1280]{1,0:T(8,128)(2,1)S(1)}, u32[]{:S(2)}, u32[]{:S(2)}) collective-permute-start(bf16[32,1280]{1,0:T(8,128)(2,1)} %get-tuple-element.43), channel_id=1, source_target_pairs={{0,17},{1,16},{2,19},{3,18},{16,1},{17,0},{18,3},{19,2},{4,21},{5,... | collective-permute-start | bytes 245768 | tf_op jit(solution)/shard_map/ppermute | solution.py:427
  10.1 7.5 %collective-permute-start.10 = (bf16[32,1280]{1,0:T(8,128)(2,1)}, bf16[32,1280]{1,0:T(8,128)(2,1)S(1)}, u32[]{:S(2)}, u32[]{:S(2)}) collective-permute-start(bf16[32,1280]{1,0:T(8,128)(2,1)} %get-tuple-element.44), channel_id=1, source_target_pairs={{0,18},{1,19},{2,16},{3,17},{16,2},{17,3},{18,0},{19,1},{4,22},{5,... | collective-permute-start | bytes 245768 | tf_op jit(solution)/shard_map/ppermute | solution.py:427
  16.8 7.4 %collective-permute-start.13 = (bf16[32,1280]{1,0:T(8,128)(2,1)}, bf16[32,1280]{1,0:T(8,128)(2,1)S(1)}, u32[]{:S(2)}, u32[]{:S(2)}) collective-permute-start(bf16[32,1280]{1,0:T(8,128)(2,1)} %get-tuple-element.48), channel_id=1, source_target_pairs={{0,3},{1,2},{2,1},{3,0},{16,19},{17,18},{18,17},{19,16},{4,7},{5,6... | collective-permute-start | bytes 245768 | tf_op jit(solution)/shard_map/ppermute | solution.py:427
  17.6 8.1 %collective-permute-start.16 = (bf16[32,1280]{1,0:T(8,128)(2,1)}, bf16[32,1280]{1,0:T(8,128)(2,1)S(1)}, u32[]{:S(2)}, u32[]{:S(2)}) collective-permute-start(bf16[32,1280]{1,0:T(8,128)(2,1)} %get-tuple-element.49), channel_id=1, source_target_pairs={{0,19},{1,18},{2,17},{3,16},{16,3},{17,2},{18,1},{19,0},{4,23},{5,... | collective-permute-start | bytes 245768 | tf_op jit(solution)/shard_map/ppermute | solution.py:427
  20.4 7.3 %collective-permute-start = (bf16[1,1,32,1280]{3,2,1,0:T(8,128)(2,1)}, bf16[1,1,32,1280]{3,2,1,0:T(8,128)(2,1)S(1)}, u32[]{:S(2)}, u32[]{:S(2)}) collective-permute-start(bf16[1,1,32,1280]{3,2,1,0:T(8,128)(2,1)} %bitcast.23), channel_id=1, source_target_pairs={{0,4},{4,0},{8,12},{12,8},{1,5},{5,1},{9,13},{13,9},{2,6},{6,2},{1... | collective-permute-start | bytes 245768 | tf_op jit(solution)/shard_map/ppermute | solution.py:431
  21.9 13.9 %collective-permute-start.3 = (bf16[1,1,32,1280]{3,2,1,0:T(8,128)(2,1)S(1)}, bf16[1,1,32,1280]{3,2,1,0:T(8,128)(2,1)S(1)}, u32[]{:S(2)}, u32[]{:S(2)}) collective-permute-start(bf16[1,1,32,1280]{3,2,1,0:T(8,128)(2,1)S(1)} %bitcast.19), channel_id=1, source_target_pairs={{0,8},{4,12},{8,0},{12,4},{1,9},{5,13},{9,1},{13,5},{2,10},{6,14},... | collective-permute-start | bytes 245768 | tf_op jit(solution)/shard_map/ppermute | solution.py:431
  24.2 12.7 %collective-permute-start.14 = (bf16[1,1,32,1280]{3,2,1,0:T(8,128)(2,1)S(1)}, bf16[1,1,32,1280]{3,2,1,0:T(8,128)(2,1)S(1)}, u32[]{:S(2)}, u32[]{:S(2)}) collective-permute-start(bf16[1,1,32,1280]{3,2,1,0:T(8,128)(2,1)S(1)} %bitcast.21), channel_id=1, source_target_pairs={{0,4},{4,0},{8,12},{12,8},{1,5},{5,1},{9,13},{13,9},{2,6},{6,2},{1... | collective-permute-start | bytes 245768 | tf_op jit(solution)/shard_map/ppermute | solution.py:431
  25.7 5.3 %collective-permute-start.17 = (bf16[1,1,32,1280]{3,2,1,0:T(8,128)(2,1)S(1)}, bf16[1,1,32,1280]{3,2,1,0:T(8,128)(2,1)S(1)}, u32[]{:S(2)}, u32[]{:S(2)}) collective-permute-start(bf16[1,1,32,1280]{3,2,1,0:T(8,128)(2,1)S(1)} %bitcast.27), channel_id=1, source_target_pairs={{0,8},{4,12},{8,0},{12,4},{1,9},{5,13},{9,1},{13,5},{2,10},{6,14},... | collective-permute-start | bytes 245768 | tf_op jit(solution)/shard_map/ppermute | solution.py:431
  27.2 7.3 %collective-permute-start.11 = (bf16[1,2,32,1280]{3,2,1,0:T(8,128)(2,1)S(1)}, bf16[1,2,32,1280]{3,2,1,0:T(8,128)(2,1)S(1)}, u32[]{:S(2)}, u32[]{:S(2)}) collective-permute-start(bf16[1,2,32,1280]{3,2,1,0:T(8,128)(2,1)S(1)} %maximum_bitcast_fusion.1), channel_id=1, source_target_pairs={{0,8},{4,12},{8,0},{12,4},{1,9},{5,13},{9,1},{13,5},{2,10},{6,14},... | collective-permute-start | bytes 491528 | tf_op jit(solution)/shard_map/ppermute | solution.py:431
  27.7 5.4 %collective-permute-start.7 = (bf16[1,2,32,1280]{3,2,1,0:T(8,128)(2,1)S(1)}, bf16[1,2,32,1280]{3,2,1,0:T(8,128)(2,1)S(1)}, u32[]{:S(2)}, u32[]{:S(2)}) collective-permute-start(bf16[1,2,32,1280]{3,2,1,0:T(8,128)(2,1)S(1)} %maximum_bitcast_fusion), channel_id=1, source_target_pairs={{0,4},{4,0},{8,12},{12,8},{1,5},{5,1},{9,13},{13,9},{2,6},{6,2},{1... | collective-permute-start | bytes 491528 | tf_op jit(solution)/shard_map/ppermute | solution.py:431
  31.0 7.1 %collective-permute-start.1 = (bf16[2,1,32,1280]{3,2,1,0:T(8,128)(2,1)S(1)}, bf16[2,1,32,1280]{3,2,1,0:T(8,128)(2,1)S(1)}, u32[]{:S(2)}, u32[]{:S(2)}) collective-permute-start(bf16[2,1,32,1280]{3,2,1,0:T(8,128)(2,1)S(1)} %pad_maximum_fusion.2.refs_0_), channel_id=1, source_target_pairs={{0,8},{4,12},{8,0},{12,4},{1,9},{5,13},{9,1},{13,5},{2,10},{6,14},... | collective-permute-start | bytes 491528 | tf_op jit(solution)/shard_map/ppermute | solution.py:431
  33.1 20.0 %collective-permute-start.18 = (bf16[2,1,32,1280]{3,2,1,0:T(8,128)(2,1)S(1)}, bf16[2,1,32,1280]{3,2,1,0:T(8,128)(2,1)S(1)}, u32[]{:S(2)}, u32[]{:S(2)}) collective-permute-start(bf16[2,1,32,1280]{3,2,1,0:T(8,128)(2,1)S(1)} %pad_maximum_fusion.5.refs_8_), channel_id=1, source_target_pairs={{0,4},{4,0},{8,12},{12,8},{1,5},{5,1},{9,13},{13,9},{2,6},{6,2},{1... | collective-permute-start | bytes 491528 | tf_op jit(solution)/shard_map/ppermute | solution.py:431
  34.5 16.0 %collective-permute-start.8 = (bf16[2,2,32,1280]{3,2,1,0:T(8,128)(2,1)S(1)}, bf16[2,2,32,1280]{3,2,1,0:T(8,128)(2,1)S(1)}, u32[]{:S(2)}, u32[]{:S(2)}) collective-permute-start(bf16[2,2,32,1280]{3,2,1,0:T(8,128)(2,1)S(1)} %pad_maximum_fusion.refs_0_), channel_id=1, source_target_pairs={{0,8},{4,12},{8,0},{12,4},{1,9},{5,13},{9,1},{13,5},{2,10},{6,14},... | collective-permute-start | bytes 983048 | tf_op jit(solution)/shard_map/ppermute | solution.py:431
  35.9 14.6 %collective-permute-start.12 = (bf16[2,2,32,1280]{3,2,1,0:T(8,128)(2,1)S(1)}, bf16[2,2,32,1280]{3,2,1,0:T(8,128)(2,1)S(1)}, u32[]{:S(2)}, u32[]{:S(2)}) collective-permute-start(bf16[2,2,32,1280]{3,2,1,0:T(8,128)(2,1)S(1)} %pad_maximum_fusion.1.refs_2_), channel_id=1, source_target_pairs={{0,4},{4,0},{8,12},{12,8},{1,5},{5,1},{9,13},{13,9},{2,6},{6,2},{1... | collective-permute-start | bytes 983048 | tf_op jit(solution)/shard_map/ppermute | solution.py:431
  36.9 12.0 %collective-permute-start.4 = (bf16[2,1,32,1280]{3,2,1,0:T(8,128)(2,1)S(1)}, bf16[2,1,32,1280]{3,2,1,0:T(8,128)(2,1)S(1)}, u32[]{:S(2)}, u32[]{:S(2)}) collective-permute-start(bf16[2,1,32,1280]{3,2,1,0:T(8,128)(2,1)S(1)} %pad_maximum_fusion.3.refs_2_), channel_id=1, source_target_pairs={{0,4},{4,0},{8,12},{12,8},{1,5},{5,1},{9,13},{13,9},{2,6},{6,2},{1... | collective-permute-start | bytes 491528 | tf_op jit(solution)/shard_map/ppermute | solution.py:431
  38.1 15.0 %collective-permute-start.15 = (bf16[2,1,32,1280]{3,2,1,0:T(8,128)(2,1)S(1)}, bf16[2,1,32,1280]{3,2,1,0:T(8,128)(2,1)S(1)}, u32[]{:S(2)}, u32[]{:S(2)}) collective-permute-start(bf16[2,1,32,1280]{3,2,1,0:T(8,128)(2,1)S(1)} %pad_maximum_fusion.4.refs_6_), channel_id=1, source_target_pairs={{0,8},{4,12},{8,0},{12,4},{1,9},{5,13},{9,1},{13,5},{2,10},{6,14},... | collective-permute-start | bytes 491528 | tf_op jit(solution)/shard_map/ppermute | solution.py:431
  50.5 2.7 %copy-start.5 = (s32[1,8]{1,0:T(1,128)S(1)}, s32[1,8]{1,0:T(1,128)}, u32[]{:S(2)}) copy-start(s32[1,8]{1,0:T(1,128)} %req_ref.3) | copy-start | bytes 100
  62.3 25.3 %copy-start.1 = (bf16[128,1280]{1,0:T(8,128)(2,1)S(1)}, bf16[128,1280]{1,0:T(8,128)(2,1)}, u32[]{:S(2)}) copy-start(bf16[128,1280]{1,0:T(8,128)(2,1)} %get-tuple-element.33.moved_ref) | copy-start | bytes 983044
  62.3 25.3 %copy-start.2 = (bf16[128,128]{1,0:T(8,128)(2,1)S(1)}, bf16[128,128]{1,0:T(8,128)(2,1)}, u32[]{:S(2)}) copy-start(bf16[128,128]{1,0:T(8,128)(2,1)} %get-tuple-element.34.lo_ref) | copy-start | bytes 98308
  62.3 25.3 %copy-start.3 = (bf16[128,128]{1,0:T(8,128)(2,1)S(1)}, bf16[128,128]{1,0:T(8,128)(2,1)}, u32[]{:S(2)}) copy-start(bf16[128,128]{1,0:T(8,128)(2,1)} %get-tuple-element.35.hi_ref) | copy-start | bytes 98308
  62.4 5.8 %collective-permute-start.19 = (bf16[4,16,640]{2,1,0:T(8,128)(2,1)S(1)}, bf16[4,16,640]{2,1,0:T(8,128)(2,1)S(1)}, u32[]{:S(2)}, u32[]{:S(2)}) collective-permute-start(bf16[4,16,640]{2,1,0:T(8,128)(2,1)S(1)} %get-tuple-element.54), channel_id=1, source_target_pairs={{0,4},{4,0},{8,12},{12,8},{1,5},{5,1},{9,13},{13,9},{2,6},{6,2},{1... | collective-permute-start | bytes 245768 | tf_op jit(solution)/shard_map/ppermute | solution.py:431
  63.5 7.0 %collective-permute-start.20 = (bf16[4,16,640]{2,1,0:T(8,128)(2,1)S(1)}, bf16[4,16,640]{2,1,0:T(8,128)(2,1)S(1)}, u32[]{:S(2)}, u32[]{:S(2)}) collective-permute-start(bf16[4,16,640]{2,1,0:T(8,128)(2,1)S(1)} %get-tuple-element.55), channel_id=1, source_target_pairs={{0,8},{4,12},{8,0},{12,4},{1,9},{5,13},{9,1},{13,5},{2,10},{6,14},... | collective-permute-start | bytes 245768 | tf_op jit(solution)/shard_map/ppermute | solution.py:431
  64.7 5.7 %collective-permute-start.21 = (bf16[4,16,640]{2,1,0:T(8,128)(2,1)S(1)}, bf16[4,16,640]{2,1,0:T(8,128)(2,1)S(1)}, u32[]{:S(2)}, u32[]{:S(2)}) collective-permute-start(bf16[4,16,640]{2,1,0:T(8,128)(2,1)S(1)} %get-tuple-element.56), channel_id=1, source_target_pairs={{0,12},{4,8},{8,4},{12,0},{1,13},{5,9},{9,5},{13,1},{2,14},{6,10},... | collective-permute-start | bytes 245768 | tf_op jit(solution)/shard_map/ppermute | solution.py:431
  66.0 6.3 %collective-permute-start.25 = (bf16[4,16,640]{2,1,0:T(8,128)(2,1)S(1)}, bf16[4,16,640]{2,1,0:T(8,128)(2,1)S(1)}, u32[]{:S(2)}, u32[]{:S(2)}) collective-permute-start(bf16[4,16,640]{2,1,0:T(8,128)(2,1)S(1)} %get-tuple-element.58), channel_id=1, source_target_pairs={{0,4},{4,0},{8,12},{12,8},{1,5},{5,1},{9,13},{13,9},{2,6},{6,2},{1... | collective-permute-start | bytes 245768 | tf_op jit(solution)/shard_map/ppermute | solution.py:431
  67.0 5.6 %collective-permute-start.26 = (bf16[4,16,640]{2,1,0:T(8,128)(2,1)S(1)}, bf16[4,16,640]{2,1,0:T(8,128)(2,1)S(1)}, u32[]{:S(2)}, u32[]{:S(2)}) collective-permute-start(bf16[4,16,640]{2,1,0:T(8,128)(2,1)S(1)} %get-tuple-element.59), channel_id=1, source_target_pairs={{0,8},{4,12},{8,0},{12,4},{1,9},{5,13},{9,1},{13,5},{2,10},{6,14},... | collective-permute-start | bytes 245768 | tf_op jit(solution)/shard_map/ppermute | solution.py:431
  68.2 5.3 %collective-permute-start.27 = (bf16[4,16,640]{2,1,0:T(8,128)(2,1)S(1)}, bf16[4,16,640]{2,1,0:T(8,128)(2,1)S(1)}, u32[]{:S(2)}, u32[]{:S(2)}) collective-permute-start(bf16[4,16,640]{2,1,0:T(8,128)(2,1)S(1)} %get-tuple-element.60), channel_id=1, source_target_pairs={{0,12},{4,8},{8,4},{12,0},{1,13},{5,9},{9,5},{13,1},{2,14},{6,10},... | collective-permute-start | bytes 245768 | tf_op jit(solution)/shard_map/ppermute | solution.py:431
  70.5 5.6 %collective-permute-start.22 = (bf16[4,16,640]{2,1,0:T(8,128)(2,1)S(1)}, bf16[4,16,640]{2,1,0:T(8,128)(2,1)S(1)}, u32[]{:S(2)}, u32[]{:S(2)}) collective-permute-start(bf16[4,16,640]{2,1,0:T(8,128)(2,1)S(1)} %pad_maximum_fusion.7), channel_id=1, source_target_pairs={{0,16},{1,17},{2,18},{3,19},{16,0},{17,1},{18,2},{19,3},{4,20},{5,... | collective-permute-start | bytes 245768 | tf_op jit(solution)/shard_map/ppermute | solution.py:427
  70.6 7.5 %collective-permute-start.23 = (bf16[4,16,640]{2,1,0:T(8,128)(2,1)S(1)}, bf16[4,16,640]{2,1,0:T(8,128)(2,1)S(1)}, u32[]{:S(2)}, u32[]{:S(2)}) collective-permute-start(bf16[4,16,640]{2,1,0:T(8,128)(2,1)S(1)} %pad_maximum_fusion.8), channel_id=1, source_target_pairs={{0,1},{1,0},{2,3},{3,2},{16,17},{17,16},{18,19},{19,18},{4,5},{5,4... | collective-permute-start | bytes 245768 | tf_op jit(solution)/shard_map/ppermute | solution.py:427
  72.3 7.7 %collective-permute-start.24 = (bf16[4,16,640]{2,1,0:T(8,128)(2,1)S(1)}, bf16[4,16,640]{2,1,0:T(8,128)(2,1)S(1)}, u32[]{:S(2)}, u32[]{:S(2)}) collective-permute-start(bf16[4,16,640]{2,1,0:T(8,128)(2,1)S(1)} %pad_maximum_fusion.9), channel_id=1, source_target_pairs={{0,17},{1,16},{2,19},{3,18},{16,1},{17,0},{18,3},{19,2},{4,21},{5,... | collective-permute-start | bytes 245768 | tf_op jit(solution)/shard_map/ppermute | solution.py:427
  73.6 12.5 %collective-permute-start.28 = (bf16[4,16,640]{2,1,0:T(8,128)(2,1)S(1)}, bf16[4,16,640]{2,1,0:T(8,128)(2,1)S(1)}, u32[]{:S(2)}, u32[]{:S(2)}) collective-permute-start(bf16[4,16,640]{2,1,0:T(8,128)(2,1)S(1)} %pad_maximum_fusion.10), channel_id=1, source_target_pairs={{0,2},{1,3},{2,0},{3,1},{16,18},{17,19},{18,16},{19,17},{4,6},{5,7... | collective-permute-start | bytes 245768 | tf_op jit(solution)/shard_map/ppermute | solution.py:427
  76.0 11.6 %collective-permute-start.29 = (bf16[4,16,640]{2,1,0:T(8,128)(2,1)S(1)}, bf16[4,16,640]{2,1,0:T(8,128)(2,1)S(1)}, u32[]{:S(2)}, u32[]{:S(2)}) collective-permute-start(bf16[4,16,640]{2,1,0:T(8,128)(2,1)S(1)} %pad_maximum_fusion.11), channel_id=1, source_target_pairs={{0,18},{1,19},{2,16},{3,17},{16,2},{17,3},{18,0},{19,1},{4,22},{5,... | collective-permute-start | bytes 245768 | tf_op jit(solution)/shard_map/ppermute | solution.py:427
  76.1 11.5 %collective-permute-start.30 = (bf16[4,16,640]{2,1,0:T(8,128)(2,1)S(1)}, bf16[4,16,640]{2,1,0:T(8,128)(2,1)S(1)}, u32[]{:S(2)}, u32[]{:S(2)}) collective-permute-start(bf16[4,16,640]{2,1,0:T(8,128)(2,1)S(1)} %pad_maximum_fusion.12), channel_id=1, source_target_pairs={{0,3},{1,2},{2,1},{3,0},{16,19},{17,18},{18,17},{19,16},{4,7},{5,6... | collective-permute-start | bytes 245768 | tf_op jit(solution)/shard_map/ppermute | solution.py:427
  78.1 9.5 %collective-permute-start.31 = (bf16[4,16,640]{2,1,0:T(8,128)(2,1)S(1)}, bf16[4,16,640]{2,1,0:T(8,128)(2,1)S(1)}, u32[]{:S(2)}, u32[]{:S(2)}) collective-permute-start(bf16[4,16,640]{2,1,0:T(8,128)(2,1)S(1)} %pad_maximum_fusion.13), channel_id=1, source_target_pairs={{0,19},{1,18},{2,17},{3,16},{16,3},{17,2},{18,1},{19,0},{4,23},{5,... | collective-permute-start | bytes 245768 | tf_op jit(solution)/shard_map/ppermute | solution.py:427

commit v2 on v1

--- a/solution.py
+++ b/solution.py
@@ -124,7 +124,7 @@
 
 SEC, LINES, PLANES = 2, 4, 4
 BLOCKS = SEC * PLANES
-GROUPS = ((0,), (1, 2), (3,))
+GROUPS = ((0,), (2,), (1, 3))
 
 
 def dot_t(a, b):
@@ -246,8 +246,8 @@
     )
 
 
-def project(pieces, gain_ref, w_ref, b_ref, kb_ref, q_ref, k_ref, v_ref, q_at, at, normed_ref):
-    planes, cap = pieces[0].shape[1:3]
+def project(pieces, gain_ref, w_ref, b_ref, kb_ref, q_ref, k_ref, v_ref, starts, normed_ref):
+    cap = pieces[0].shape[2]
     cols = w_ref.shape[1]
     heads = cols // HD
     block_rows = LINES * cap
@@ -258,7 +258,7 @@
         row = jnp.pad(b_ref[part : part + 1, :].astype(jnp.float32), ((0, 0), (0, -cols % LANES)))
         column = jnp.broadcast_to(row, (LANES, row.shape[1])).T[:cols]
         columns.append(jnp.concatenate([column] * (SEC * block_rows // LANES), axis=1))
-    for j in range(planes):
+    for j, at in enumerate(starts):
         for r in range(SEC):
             for step in range(2):
                 for n in range(2):
@@ -269,31 +269,32 @@
                     normed = (wide * lax.rsqrt(mean_sq + NORM_EPS) * gain_ref[...]).astype(jnp.bfloat16)
                     normed_ref[(r * LINES + m) * cap : (r * LINES + m + 1) * cap, :] = normed
                     flag = iota((cap, heads * LANES), 1) % LANES == HD
-                    b = at + SEC * j + r
-                    k_ref[b, m * cap : (m + 1) * cap, :] = jnp.where(flag, shut, 0.0).astype(jnp.bfloat16)
+                    k_ref[at + r, m * cap : (m + 1) * cap, :] = jnp.where(flag, shut, 0.0).astype(jnp.bfloat16)
         rows = normed_ref[...]
         q = (dot_t(w_ref[0], rows) + columns[0]).astype(jnp.bfloat16)
         v = (dot_t(w_ref[2], rows) + columns[1]).astype(jnp.bfloat16)
         for r in range(SEC):
             span = slice(r * block_rows, (r + 1) * block_rows)
-            v_ref[at + SEC * j + r] = v[:, span]
+            v_ref[at + r] = v[:, span]
             for head in range(heads):
-                q_ref[q_at + SEC * j + r, head, :HD, :] = q[head * HD : (head + 1) * HD, span]
-                q_ref[q_at + SEC * j + r, head, HD:, :] = tail
+                q_ref[at + r, head, :HD, :] = q[head * HD : (head + 1) * HD, span]
+                q_ref[at + r, head, HD:, :] = tail
         for head in range(heads):
             k = dot_t(rows, w_ref[1, head * HD : (head + 1) * HD, :]) + kb_ref[head : head + 1, :]
             k = k.astype(jnp.bfloat16)
             for r in range(SEC):
                 span = slice(r * block_rows, (r + 1) * block_rows)
-                k_ref[at + SEC * j + r, :, head * LANES : head * LANES + HD] = k[span]
+                k_ref[at + r, :, head * LANES : head * LANES + HD] = k[span]
 
 
 def project_kernel(*refs):
     pieces, (gain_ref, w_ref, b_ref, kb_ref, q_ref, k_ref, v_ref, normed_ref) = refs[:4], refs[4:]
-    project(pieces, gain_ref, w_ref, b_ref, kb_ref, q_ref, k_ref, v_ref, 0, 0, normed_ref)
-
-
-def attend(req_ref, q_ref, k_ref, v_ref, first_block, out_refs, score_ref):
+    planes = pieces[0].shape[1]
+    starts = range(0, SEC * planes, SEC)
+    project(pieces, gain_ref, w_ref, b_ref, kb_ref, q_ref, k_ref, v_ref, starts, normed_ref)
+
+
+def attend(req_ref, q_ref, k_ref, v_ref, first_block, out_refs, score_ref, mixed_ref):
     dev, sec = lax.axis_index("dev"), lax.axis_index("sec")
     heads = q_ref.shape[1]
     cols, block_rows = v_ref.shape[1:]
@@ -301,11 +302,15 @@
     half = group // 2
     most = BLOCKS // 2
 
+    if cols % LANES:
+        mixed_ref[cols:, :] = jnp.zeros((-cols % LANES, block_rows), jnp.float32)
+
     def block_of(position):
         return ((position & (PLANES - 1)) ^ dev) * SEC + ((position // PLANES) ^ sec)
 
     def one(at, keys):
         mixed, tops, sums = [], [], []
+        emit(jnp.maximum(at - 1, 0))
         size = len(keys) * block_rows
         for head in range(heads):
             span = slice(head * LANES, (head + 1) * LANES)
@@ -329,9 +334,11 @@
             span = slice(head * HD, (head + 1) * HD)
             values = jnp.concatenate([v_ref[key, span, :] for key in keys], axis=1)
             mixed.append(dot_n(values, weights))
-        if cols % LANES:
-            mixed.append(jnp.zeros((-cols % LANES, block_rows), jnp.float32))
-        plain = jnp.concatenate(mixed, axis=0).T
+        for head in range(heads):
+            mixed_ref[head * HD : (head + 1) * HD, :] = mixed[head]
+
+    def emit(at):
+        plain = mixed_ref[...].T
         moved = pltpu.roll(plain, cols % LANES, 1)
         whole = cols // LANES
         for m in range(LINES):
@@ -364,26 +371,28 @@
         def _():
             one(at, keys)
 
+    emit(out_refs[0].shape[0] - 1)
+
 
 def attend_far_kernel(groups, req_ref, *refs):
     early = groups[:-1]
     ready, refs = refs[: 3 * len(early)], refs[3 * len(early) :]
     pieces, shared, refs = refs[:4], refs[4:8], refs[8:]
-    out_refs, (q_ref, k_ref, v_ref, normed_ref, score_ref) = refs[:LINES], refs[LINES:]
-    last = SEC * groups[-1][0]
-    project(pieces, *shared, q_ref, k_ref, v_ref, last, last, normed_ref)
+    out_refs, (q_ref, k_ref, v_ref, normed_ref, score_ref, mixed_ref) = refs[:LINES], refs[LINES:]
+    starts = [SEC * j for j in groups[-1]]
     for i, planes in enumerate(early):
-        span = slice(SEC * planes[0], SEC * (planes[-1] + 1))
         for ref, part in zip((q_ref, k_ref, v_ref), ready[3 * i : 3 * i + 3]):
-            ref[span] = part[...]
+            for n, j in enumerate(planes):
+                ref[SEC * j : SEC * (j + 1)] = part[SEC * n : SEC * (n + 1)]
     flag = iota(k_ref.shape[1:], 1) % LANES == HD
     k_ref[BLOCKS] = jnp.where(flag, NEG, 0.0).astype(jnp.bfloat16)
     v_ref[BLOCKS] = jnp.zeros(v_ref.shape[1:], jnp.bfloat16)
-    attend(req_ref, q_ref, k_ref, v_ref, BLOCKS // 2, out_refs, score_ref)
+    project(pieces, *shared, q_ref, k_ref, v_ref, starts, normed_ref)
+    attend(req_ref, q_ref, k_ref, v_ref, BLOCKS // 2, out_refs, score_ref, mixed_ref)
 
 
 def attend_near_kernel(req_ref, q_ref, k_ref, v_ref, *refs):
-    attend(req_ref, q_ref, k_ref, v_ref, 0, refs[:LINES], refs[LINES])
+    attend(req_ref, q_ref, k_ref, v_ref, 0, refs[:LINES], *refs[LINES:])
 
 
 def finish_kernel(moved_ref, lo_ref, hi_ref, *refs):
@@ -500,12 +509,13 @@
     q_store = stores(BLOCKS, block_rows, cols)[0]
     _, k_store, v_store = stores(BLOCKS + 1, block_rows, cols)
     scores = pltpu.VMEM((heads, BLOCKS // 2 * block_rows, block_rows), jnp.float32)
+    sums = pltpu.VMEM((-(-cols // LANES) * LANES, block_rows), jnp.float32)
     *far_mixed, queries, keys, values = pl.pallas_call(
         functools.partial(attend_far_kernel, GROUPS),
         out_shape=[kept((BLOCKS // 2, half, 2 * cols))] * LINES + [kept(q_store), kept(k_store), kept(v_store)],
         in_specs=[smem()] + [vmem()] * (len(ready) + 8),
         out_specs=[vmem()] * (LINES + 3),
-        scratch_shapes=[pltpu.VMEM((SEC * block_rows, width), jnp.bfloat16), scores],
+        scratch_shapes=[pltpu.VMEM((SEC * block_rows, width), jnp.bfloat16), scores, sums],
         name="attend_far",
         compiler_params=room(20),
     )(source_request, *ready, *gathered[-1], *shared)
@@ -514,7 +524,7 @@
         out_shape=[kept((BLOCKS // 2, half, 2 * cols))] * LINES,
         in_specs=[smem()] + [vmem()] * 3,
         out_specs=[vmem()] * LINES,
-        scratch_shapes=[scores],
+        scratch_shapes=[scores, sums],
         name="attend_near",
         compiler_params=room(12),
         cost_estimate=pl.CostEstimate(flops=4 << 30, bytes_accessed=6 << 20, transcendentals=2 << 20),

time: 90.5 us -> 86.8 us (0.959)
  the two profiles are of different devices: /device:TPU:0 before, /device:TPU:9 now
where the time goes in v2:
time: 86.8 us; the launch traced here: 86.5 us
  starting transfers between devices  38.1 us (44%)
  waiting for transfers between devices  23.5 us (27%)
  Pallas kernels  20.2 us (23%)
  other arithmetic  2.52 us (3%)
  local copies, waits for them, and re-layouts  1.76 us (2%)
    ppermute x14, starting transfers between devices, to_block(): return lax.ppermute(x, ('sec', 'dev'), pairs)  21.4 us
    ppermute x14, waiting for transfers between devices, to_block(): return lax.ppermute(x, ('sec', 'dev'), pairs)  17.4 us
    ppermute x18, starting transfers between devices, to_line(): return lax.ppermute(x, 'sp', [(i, i ^ m) for i in range(LINES)])  16.7 us
    pallas_call x1, Pallas kernels, shards_here(): pl.pallas_call(functools.partial(attend_far_kernel, GROUPS), out_shape=[k...  6.41 us
    ppermute x18, waiting for transfers between devices, to_line(): return lax.ppermute(x, 'sp', [(i, i ^ m) for i in range(LINES)])  6.13 us
    pallas_call x2, Pallas kernels, projected(): pl.pallas_call(project_kernel, out_shape=[kept(shape) for shape in stores...  5.01 us
    pallas_call x1, Pallas kernels, shards_here(): pl.pallas_call(window_kernel, out_shape=[kept((rows, width)), kept((rows,...  4.3 us
    pallas_call x1, Pallas kernels, shards_here(): pl.pallas_call(attend_near_kernel, out_shape=[kept((BLOCKS // 2, half, 2...  3.23 us
  transfers between devices with their start and end apart: 32, of which 10 were waited for; matrix products, arithmetic and copies ran while one was open for 3% of the time, Pallas kernels for 6%

profile of v2, /device:TPU:9, one launch (start us, length us, event | category | flops | bytes accessed | tf_op | source)
XLA Modules:
  0.0 86.5 jit_solution(5475351664599312093)
XLA Ops:
  0.0 4.3 %window.1 = (bf16[128,1280]{1,0:T(8,128)(2,1)}, bf16[128,128]{1,0:T(8,128)(2,1)}, bf16[128,128]{1,0:T(8,128)(2,1)}, bf16[32,1280]{1,0:T(8,128)(2,1)}, bf16[32,12...) custom-call(bf16[3,128,1280]{2,1,0:T(8,128)(2,1)} %bitcast.18, ...), custom_call_target="tpu_custom_call" | custom-call | tf_op jit(solution)/shard_map/window/pallas_call | solution.py:465
  4.3 0.1 collective-permute-start.15
  4.4 2.9 %collective-permute-start.16 = (bf16[32,1280]{1,0:T(8,128)(2,1)}, bf16[32,1280]{1,0:T(8,128)(2,1)S(1)}, u32[]{:S(2)}, u32[]{:S(2)}) collective-permute-start(bf16[32,1280]{1,0:T(8,128)(2,1)} %get-tuple-element.49), channel_id=1, source_target_pairs={{0,19},{1,18},{2,17},{3,16},{16,3},{17,2},{18,1},{19,0},{4,23},{5,... | collective-permute-start | bytes 245768 | tf_op jit(solution)/shard_map/ppermute | solution.py:436
  7.3 0.7 collective-permute-start.2
  7.9 1.0 %collective-permute-start.5 = (bf16[32,1280]{1,0:T(8,128)(2,1)}, bf16[32,1280]{1,0:T(8,128)(2,1)S(1)}, u32[]{:S(2)}, u32[]{:S(2)}) collective-permute-start(bf16[32,1280]{1,0:T(8,128)(2,1)} %get-tuple-element.41), channel_id=1, source_target_pairs={{0,2},{1,3},{2,0},{3,1},{16,18},{17,19},{18,16},{19,17},{4,6},{5,7... | collective-permute-start | bytes 245768 | tf_op jit(solution)/shard_map/ppermute | solution.py:436
  8.9 1.6 %collective-permute-start.8 = (bf16[32,1280]{1,0:T(8,128)(2,1)}, bf16[32,1280]{1,0:T(8,128)(2,1)S(1)}, u32[]{:S(2)}, u32[]{:S(2)}) collective-permute-start(bf16[32,1280]{1,0:T(8,128)(2,1)} %get-tuple-element.42), channel_id=1, source_target_pairs={{0,18},{1,19},{2,16},{3,17},{16,2},{17,3},{18,0},{19,1},{4,22},{5,... | collective-permute-start | bytes 245768 | tf_op jit(solution)/shard_map/ppermute | solution.py:436
  10.5 0.0 collective-permute-done.15
  10.5 1.1 %collective-permute-start.11 = (bf16[32,1280]{1,0:T(8,128)(2,1)}, bf16[32,1280]{1,0:T(8,128)(2,1)S(1)}, u32[]{:S(2)}, u32[]{:S(2)}) collective-permute-start(bf16[32,1280]{1,0:T(8,128)(2,1)} %get-tuple-element.46), channel_id=1, source_target_pairs={{0,1},{1,0},{2,3},{3,2},{16,17},{17,16},{18,19},{19,18},{4,5},{5,4... | collective-permute-start | bytes 245768 | tf_op jit(solution)/shard_map/ppermute | solution.py:436
  11.6 4.4 %collective-permute-done.16 = bf16[32,1280]{1,0:T(8,128)(2,1)S(1)} collective-permute-done((bf16[32,1280]{1,0:T(8,128)(2,1)}, bf16[32,1280]{1,0:T(8,128)(2,1)S(1)}, u32[]{:S(2)}, u32[]{:S(2)}) %collective-permute-start.16) | collective-permute-done | bytes 81952 | tf_op jit(solution)/shard_map/ppermute | solution.py:436
  16.0 1.9 %collective-permute-start.12 = (bf16[32,1280]{1,0:T(8,128)(2,1)}, bf16[32,1280]{1,0:T(8,128)(2,1)S(1)}, u32[]{:S(2)}, u32[]{:S(2)}) collective-permute-start(bf16[32,1280]{1,0:T(8,128)(2,1)} %get-tuple-element.47), channel_id=1, source_target_pairs={{0,3},{1,2},{2,1},{3,0},{16,19},{17,18},{18,17},{19,16},{4,7},{5,6... | collective-permute-start | bytes 245768 | tf_op jit(solution)/shard_map/ppermute | solution.py:436
  17.9 0.0 collective-permute-done.2
  17.9 1.3 %collective-permute-start = (bf16[1,1,32,1280]{3,2,1,0:T(8,128)(2,1)}, bf16[1,1,32,1280]{3,2,1,0:T(8,128)(2,1)S(1)}, u32[]{:S(2)}, u32[]{:S(2)}) collective-permute-start(bf16[1,1,32,1280]{3,2,1,0:T(8,128)(2,1)} %bitcast.21), channel_id=1, source_target_pairs={{0,4},{4,0},{8,12},{12,8},{1,5},{5,1},{9,13},{13,9},{2,6},{6,2},{1... | collective-permute-start | bytes 245768 | tf_op jit(solution)/shard_map/ppermute | solution.py:440
  19.2 1.2 %collective-permute-start.3 = (bf16[1,1,32,1280]{3,2,1,0:T(8,128)(2,1)S(1)}, bf16[1,1,32,1280]{3,2,1,0:T(8,128)(2,1)S(1)}, u32[]{:S(2)}, u32[]{:S(2)}) collective-permute-start(bf16[1,1,32,1280]{3,2,1,0:T(8,128)(2,1)S(1)} %bitcast.19), channel_id=1, source_target_pairs={{0,8},{4,12},{8,0},{12,4},{1,9},{5,13},{9,1},{13,5},{2,10},{6,14},... | collective-permute-start | bytes 245768 | tf_op jit(solution)/shard_map/ppermute | solution.py:440
  20.4 0.0 collective-permute-done.8
  20.4 0.5 collective-permute-start.6
  20.9 0.0 collective-permute-done.11
  20.9 1.2 %collective-permute-start.9 = (bf16[1,1,32,1280]{3,2,1,0:T(8,128)(2,1)S(1)}, bf16[1,1,32,1280]{3,2,1,0:T(8,128)(2,1)S(1)}, u32[]{:S(2)}, u32[]{:S(2)}) collective-permute-start(bf16[1,1,32,1280]{3,2,1,0:T(8,128)(2,1)S(1)} %bitcast.25), channel_id=1, source_target_pairs={{0,8},{4,12},{8,0},{12,4},{1,9},{5,13},{9,1},{13,5},{2,10},{6,14},... | collective-permute-start | bytes 245768 | tf_op jit(solution)/shard_map/ppermute | solution.py:440
  22.1 0.9 %collective-permute-done.12 = bf16[32,1280]{1,0:T(8,128)(2,1)S(1)} collective-permute-done((bf16[32,1280]{1,0:T(8,128)(2,1)}, bf16[32,1280]{1,0:T(8,128)(2,1)S(1)}, u32[]{:S(2)}, u32[]{:S(2)}) %collective-permute-start.12) | collective-permute-done | bytes 81952 | tf_op jit(solution)/shard_map/ppermute | solution.py:436
  23.0 1.2 %collective-permute-start.17 = (bf16[1,2,32,1280]{3,2,1,0:T(8,128)(2,1)S(1)}, bf16[1,2,32,1280]{3,2,1,0:T(8,128)(2,1)S(1)}, u32[]{:S(2)}, u32[]{:S(2)}) collective-permute-start(bf16[1,2,32,1280]{3,2,1,0:T(8,128)(2,1)S(1)} %maximum_bitcast_fusion.1), channel_id=1, source_target_pairs={{0,8},{4,12},{8,0},{12,4},{1,9},{5,13},{9,1},{13,5},{2,10},{6,14},... | collective-permute-start | bytes 491528 | tf_op jit(solution)/shard_map/ppermute | solution.py:440
  24.3 0.0 collective-permute-done
  24.3 1.3 %collective-permute-start.13 = (bf16[1,2,32,1280]{3,2,1,0:T(8,128)(2,1)S(1)}, bf16[1,2,32,1280]{3,2,1,0:T(8,128)(2,1)S(1)}, u32[]{:S(2)}, u32[]{:S(2)}) collective-permute-start(bf16[1,2,32,1280]{3,2,1,0:T(8,128)(2,1)S(1)} %maximum_bitcast_fusion), channel_id=1, source_target_pairs={{0,4},{4,0},{8,12},{12,8},{1,5},{5,1},{9,13},{13,9},{2,6},{6,2},{1... | collective-permute-start | bytes 491528 | tf_op jit(solution)/shard_map/ppermute | solution.py:440
  25.6 0.9 %pad_maximum_fusion.2.refs_0_ = bf16[2,1,32,1280]{3,2,1,0:T(8,128)(2,1)S(1)} fusion(bf16[1,1,32,1280]{3,2,1,0:T(8,128)(2,1)S(1)} %collective-permute-done, bf16[1,1,32,1280]{3,2,1,0:T(8,128)(2,1)} %bitcast.22), kind=kLoop, calls=%fused_computation.2 | loop fusion | flops 81920 | bytes 327680 | tf_op jit(solution)/shard_map/concatenate | solution.py:446
  26.5 0.3 collective-permute-start.1
  26.8 0.0 collective-permute-done.6
  26.8 0.3 collective-permute-start.10
  27.1 0.7 pad_maximum_fusion.4.refs_0_
  27.8 1.6 %collective-permute-done.13 = bf16[1,2,32,1280]{3,2,1,0:T(8,128)(2,1)S(1)} collective-permute-done((bf16[1,2,32,1280]{3,2,1,0:T(8,128)(2,1)S(1)}, bf16[1,2,32,1280]{3,2,1,0:T(8,128)(2,1)S(1)}, u32[]{:S(2)}, u32[]{:S(2)}) %collective-permute-start.13) | collective-permute-done | bytes 163872 | tf_op jit(solution)/shard_map/ppermute | solution.py:440
  29.4 0.0 collective-permute-done.17
  29.5 1.5 %collective-permute-start.14 = (bf16[2,2,32,1280]{3,2,1,0:T(8,128)(2,1)S(1)}, bf16[2,2,32,1280]{3,2,1,0:T(8,128)(2,1)}, u32[]{:S(2)}, u32[]{:S(2)}) collective-permute-start(bf16[2,2,32,1280]{3,2,1,0:T(8,128)(2,1)S(1)} %pad_maximum_fusion.refs_6_), channel_id=1, source_target_pairs={{0,8},{4,12},{8,0},{12,4},{1,9},{5,13},{9,1},{13,5},{2,10},{6,14},... | collective-permute-start | bytes 983048 | tf_op jit(solution)/shard_map/ppermute | solution.py:440
  31.0 1.3 %collective-permute-start.18 = (bf16[2,2,32,1280]{3,2,1,0:T(8,128)(2,1)S(1)}, bf16[2,2,32,1280]{3,2,1,0:T(8,128)(2,1)}, u32[]{:S(2)}, u32[]{:S(2)}) collective-permute-start(bf16[2,2,32,1280]{3,2,1,0:T(8,128)(2,1)S(1)} %pad_maximum_fusion.1.refs_8_), channel_id=1, source_target_pairs={{0,4},{4,0},{8,12},{12,8},{1,5},{5,1},{9,13},{13,9},{2,6},{6,2},{1... | collective-permute-start | bytes 983048 | tf_op jit(solution)/shard_map/ppermute | solution.py:440
  32.3 0.7 pad_maximum_fusion.3.refs_2_
  33.0 0.0 collective-permute-done.10.refs_3_
  33.0 0.7 copy-done.2
  33.7 1.3 %collective-permute-start.4 = (bf16[2,1,32,1280]{3,2,1,0:T(8,128)(2,1)}, bf16[2,1,32,1280]{3,2,1,0:T(8,128)(2,1)}, u32[]{:S(2)}, u32[]{:S(2)}) collective-permute-start(bf16[2,1,32,1280]{3,2,1,0:T(8,128)(2,1)} %pad_maximum_fusion.3.refs_2_), channel_id=1, source_target_pairs={{0,4},{4,0},{8,12},{12,8},{1,5},{5,1},{9,13},{13,9},{2,6},{6,2},{1... | collective-permute-start | bytes 491528 | tf_op jit(solution)/shard_map/ppermute | solution.py:440
  34.9 0.1 reshape.12.refs_7_.refs_13_
  35.0 0.5 collective-permute-done.7.refs_1_
  35.5 0.9 %copy-done.3 = bf16[2,1,32,1280]{3,2,1,0:T(8,128)(2,1)S(1)} copy-done((bf16[2,1,32,1280]{3,2,1,0:T(8,128)(2,1)S(1)}, bf16[2,1,32,1280]{3,2,1,0:T(8,128)(2,1)}, u32[]{:S(2)}) %copy-start.3) | copy-done | bytes 163864
  36.5 2.5 %project.3 = (bf16[2,4,128,128]{3,2,1,0:T(8,128)(2,1)S(1)}, bf16[2,128,512]{2,1,0:T(8,128)(2,1)S(1)}, bf16[2,320,128]{2,1,0:T(8,128)(2,1)S(1)}) custom-call(bf16[2,1,32,1280]{3,2,1,0:T(8,128)(2,1)} %pad_maximum_fusion.4.refs_0_, bf16[2,1,32,1280]{3,2,1,0:T(8,128)(2,1)} %collective-permute-done.7.refs_1_, ...), custom_call_target="tpu_custom_call" | custom-call | flops 838860800 | bytes 4194304 | tf_op jit(solution)/shard_map/project/pallas_call | solution.py:493
  38.9 0.0 collective-permute-done.1.refs_1_
  38.9 3.9 %collective-permute-done.4.refs_3_ = bf16[2,1,32,1280]{3,2,1,0:T(8,128)(2,1)} collective-permute-done((bf16[2,1,32,1280]{3,2,1,0:T(8,128)(2,1)}, bf16[2,1,32,1280]{3,2,1,0:T(8,128)(2,1)}, u32[]{:S(2)}, u32[]{:S(2)}) %collective-permute-start.4) | collective-permute-done | bytes 163872 | tf_op jit(solution)/shard_map/ppermute | solution.py:440
  42.8 2.5 %project.2 = (bf16[2,4,128,128]{3,2,1,0:T(8,128)(2,1)S(1)}, bf16[2,128,512]{2,1,0:T(8,128)(2,1)S(1)}, bf16[2,320,128]{2,1,0:T(8,128)(2,1)S(1)}) custom-call(bf16[2,1,32,1280]{3,2,1,0:T(8,128)(2,1)S(1)} %pad_maximum_fusion.2.refs_0_, bf16[2,1,32,1280]{3,2,1,0:T(8,128)(2,1)} %collective-permute-done.1.refs_1_, ...), custom_call_target="tpu_custom_call" | custom-call | flops 838860800 | bytes 4194304 | tf_op jit(solution)/shard_map/project/pallas_call | solution.py:493
  45.4 6.4 %attend_far.1 = (bf16[4,16,640]{2,1,0:T(8,128)(2,1)S(1)}, bf16[4,16,640]{2,1,0:T(8,128)(2,1)S(1)}, bf16[4,16,640]{2,1,0:T(8,128)(2,1)S(1)}, bf16[4,16,640]{2,1,0...) custom-call(s32[1,8]{1,0:T(1,128)S(1)} %copy-done.7, ...), custom_call_target="tpu_custom_call" | custom-call | tf_op jit(solution)/shard_map/attend_far/pallas_call | solution.py:513
  51.8 3.2 %attend_near.1 = (bf16[4,16,640]{2,1,0:T(8,128)(2,1)S(1)}, bf16[4,16,640]{2,1,0:T(8,128)(2,1)S(1)}, bf16[4,16,640]{2,1,0:T(8,128)(2,1)S(1)}, bf16[4,16,640]{2,1,0:T(8,128)(2,1)S(1)}) custom-call(s32[1,8]{1,0:T(1,128)S(1)} %copy-done.7, bf16[8,4,128,128]{3,2,1,0:T(8,128)(2,1)S(1)} %get-tuple-element.50.q_ref, ...), custom_call_target="tpu_custom_call" | custom-call | flops 4294967296 | bytes 6291456 | tf_op jit(solution)/shard_map/attend_near/pallas_call | solution.py:522
  55.1 0.0 copy-start.1
  55.1 0.1 collective-permute-start.19
  55.2 0.5 collective-permute-start.20
  55.7 2.2 %collective-permute-start.21 = (bf16[4,16,640]{2,1,0:T(8,128)(2,1)S(1)}, bf16[4,16,640]{2,1,0:T(8,128)(2,1)S(1)}, u32[]{:S(2)}, u32[]{:S(2)}) collective-permute-start(bf16[4,16,640]{2,1,0:T(8,128)(2,1)S(1)} %get-tuple-element.56), channel_id=1, source_target_pairs={{0,12},{4,8},{8,4},{12,0},{1,13},{5,9},{9,5},{13,1},{2,14},{6,10},... | collective-permute-start | bytes 245768 | tf_op jit(solution)/shard_map/ppermute | solution.py:440
  57.9 0.0 collective-permute-start.25
  57.9 0.4 collective-permute-start.26
  58.4 0.1 collective-permute-done.19
  58.5 2.1 %collective-permute-start.27 = (bf16[4,16,640]{2,1,0:T(8,128)(2,1)S(1)}, bf16[4,16,640]{2,1,0:T(8,128)(2,1)S(1)}, u32[]{:S(2)}, u32[]{:S(2)}) collective-permute-start(bf16[4,16,640]{2,1,0:T(8,128)(2,1)S(1)} %get-tuple-element.60), channel_id=1, source_target_pairs={{0,12},{4,8},{8,4},{12,0},{1,13},{5,9},{9,5},{13,1},{2,14},{6,10},... | collective-permute-start | bytes 245768 | tf_op jit(solution)/shard_map/ppermute | solution.py:440
  60.6 0.0 collective-permute-done.20
  60.7 4.8 %collective-permute-start.22 = (bf16[4,16,640]{2,1,0:T(8,128)(2,1)S(1)}, bf16[4,16,640]{2,1,0:T(8,128)(2,1)S(1)}, u32[]{:S(2)}, u32[]{:S(2)}) collective-permute-start(bf16[4,16,640]{2,1,0:T(8,128)(2,1)S(1)} %pad_maximum_fusion.7), channel_id=1, source_target_pairs={{0,16},{1,17},{2,18},{3,19},{16,0},{17,1},{18,2},{19,3},{4,20},{5,... | collective-permute-start | bytes 245768 | tf_op jit(solution)/shard_map/ppermute | solution.py:436
  65.4 1.5 %collective-permute-start.23 = (bf16[4,16,640]{2,1,0:T(8,128)(2,1)S(1)}, bf16[4,16,640]{2,1,0:T(8,128)(2,1)S(1)}, u32[]{:S(2)}, u32[]{:S(2)}) collective-permute-start(bf16[4,16,640]{2,1,0:T(8,128)(2,1)S(1)} %pad_maximum_fusion.8), channel_id=1, source_target_pairs={{0,1},{1,0},{2,3},{3,2},{16,17},{17,16},{18,19},{19,18},{4,5},{5,4... | collective-permute-start | bytes 245768 | tf_op jit(solution)/shard_map/ppermute | solution.py:436
  66.9 0.6 collective-permute-start.24
  67.6 1.9 %collective-permute-start.28 = (bf16[4,16,640]{2,1,0:T(8,128)(2,1)S(1)}, bf16[4,16,640]{2,1,0:T(8,128)(2,1)S(1)}, u32[]{:S(2)}, u32[]{:S(2)}) collective-permute-start(bf16[4,16,640]{2,1,0:T(8,128)(2,1)S(1)} %pad_maximum_fusion.10), channel_id=1, source_target_pairs={{0,2},{1,3},{2,0},{3,1},{16,18},{17,19},{18,16},{19,17},{4,6},{5,7... | collective-permute-start | bytes 245768 | tf_op jit(solution)/shard_map/ppermute | solution.py:436
  69.5 1.9 %collective-permute-start.29 = (bf16[4,16,640]{2,1,0:T(8,128)(2,1)S(1)}, bf16[4,16,640]{2,1,0:T(8,128)(2,1)S(1)}, u32[]{:S(2)}, u32[]{:S(2)}) collective-permute-start(bf16[4,16,640]{2,1,0:T(8,128)(2,1)S(1)} %pad_maximum_fusion.11), channel_id=1, source_target_pairs={{0,18},{1,19},{2,16},{3,17},{16,2},{17,3},{18,0},{19,1},{4,22},{5,... | collective-permute-start | bytes 245768 | tf_op jit(solution)/shard_map/ppermute | solution.py:436
  71.4 0.4 collective-permute-start.30
  71.8 1.3 %collective-permute-start.31 = (bf16[4,16,640]{2,1,0:T(8,128)(2,1)S(1)}, bf16[4,16,640]{2,1,0:T(8,128)(2,1)S(1)}, u32[]{:S(2)}, u32[]{:S(2)}) collective-permute-start(bf16[4,16,640]{2,1,0:T(8,128)(2,1)S(1)} %pad_maximum_fusion.13), channel_id=1, source_target_pairs={{0,19},{1,18},{2,17},{3,16},{16,3},{17,2},{18,1},{19,0},{4,23},{5,... | collective-permute-start | bytes 245768 | tf_op jit(solution)/shard_map/ppermute | solution.py:436
  73.1 0.4 collective-permute-done.28.refs_4_
  73.6 6.1 %collective-permute-done.29.refs_5_ = bf16[4,16,640]{2,1,0:T(8,128)(2,1)S(1)} collective-permute-done((bf16[4,16,640]{2,1,0:T(8,128)(2,1)S(1)}, bf16[4,16,640]{2,1,0:T(8,128)(2,1)S(1)}, u32[]{:S(2)}, u32[]{:S(2)}) %collective-permute-start.29) | collective-permute-done | bytes 81952 | tf_op jit(solution)/shard_map/ppermute | solution.py:436
  79.7 2.8 %collective-permute-done.30.refs_6_ = bf16[4,16,640]{2,1,0:T(8,128)(2,1)S(1)} collective-permute-done((bf16[4,16,640]{2,1,0:T(8,128)(2,1)S(1)}, bf16[4,16,640]{2,1,0:T(8,128)(2,1)S(1)}, u32[]{:S(2)}, u32[]{:S(2)}) %collective-permute-start.30) | collective-permute-done | bytes 81952 | tf_op jit(solution)/shard_map/ppermute | solution.py:436
  82.5 2.7 %collective-permute-done.31.refs_7_ = bf16[4,16,640]{2,1,0:T(8,128)(2,1)S(1)} collective-permute-done((bf16[4,16,640]{2,1,0:T(8,128)(2,1)S(1)}, bf16[4,16,640]{2,1,0:T(8,128)(2,1)S(1)}, u32[]{:S(2)}, u32[]{:S(2)}) %collective-permute-start.31) | collective-permute-done | bytes 81952 | tf_op jit(solution)/shard_map/ppermute | solution.py:436
  85.2 1.3 %finish.1 = bf16[128,1280]{1,0:T(8,128)(2,1)} custom-call(bf16[128,1280]{1,0:T(8,128)(2,1)S(1)} %copy-done.1, bf16[128,128]{1,0:T(8,128)(2,1)S(1)} %copy-done.5, bf16[128,128]{1,0:T(8,128)(2,1)S(1)} %copy-done.6, bf16[4,16,640]{2,1,0:T(8,128)(2,1)S(1)} %pad_maximum_fusion.6.refs_0_, bf16[4,16,640]{2,1,0:T(8,128)(2,1)S(1)} %collective-permute-done.22.refs_1_, ...), custom_call_target="tpu_custom_call" | custom-call | tf_op jit(solution)/shard_map/finish/pallas_call | solution.py:541
  (51 shorter events, 0.4 us)
Async XLA Ops:
  0.0 34.9 %copy-start.4 = (bf16[3,320]{1,0:T(4,128)(2,1)S(1)}, bf16[3,320]{1,0:T(4,128)(2,1)}, u32[]{:S(2)}) copy-start(bf16[3,320]{1,0:T(4,128)(2,1)} %refs_12_.1) | copy-start | bytes 5764
  0.0 35.0 %copy-start.8 = (f32[1280]{0:T(1024)S(1)}, f32[1280]{0:T(1024)}, u32[]{:S(2)}) copy-start(f32[1280]{0:T(1024)} %param.13) | copy-start | bytes 15364
  0.0 35.5 %copy-start = (bf16[1280,3,320]{0,2,1:T(8,128)(2,1)S(1)}, bf16[1280,3,320]{0,2,1:T(8,128)(2,1)}, u32[]{:S(2)}) copy-start(bf16[1280,3,320]{0,2,1:T(8,128)(2,1)} %param.14) | copy-start | bytes 7372804
  4.3 6.2 %collective-permute-start.15 = (bf16[32,1280]{1,0:T(8,128)(2,1)}, bf16[32,1280]{1,0:T(8,128)(2,1)S(1)}, u32[]{:S(2)}, u32[]{:S(2)}) collective-permute-start(bf16[32,1280]{1,0:T(8,128)(2,1)} %get-tuple-element.48), channel_id=1, source_target_pairs={{0,17},{1,16},{2,19},{3,18},{16,1},{17,0},{18,3},{19,2},{4,21},{5,... | collective-permute-start | bytes 245768 | tf_op jit(solution)/shard_map/ppermute | solution.py:436
  4.4 11.6 %collective-permute-start.16 = (bf16[32,1280]{1,0:T(8,128)(2,1)}, bf16[32,1280]{1,0:T(8,128)(2,1)S(1)}, u32[]{:S(2)}, u32[]{:S(2)}) collective-permute-start(bf16[32,1280]{1,0:T(8,128)(2,1)} %get-tuple-element.49), channel_id=1, source_target_pairs={{0,19},{1,18},{2,17},{3,16},{16,3},{17,2},{18,1},{19,0},{4,23},{5,... | collective-permute-start | bytes 245768 | tf_op jit(solution)/shard_map/ppermute | solution.py:436
  7.3 10.6 %collective-permute-start.2 = (bf16[32,1280]{1,0:T(8,128)(2,1)}, bf16[32,1280]{1,0:T(8,128)(2,1)S(1)}, u32[]{:S(2)}, u32[]{:S(2)}) collective-permute-start(bf16[32,1280]{1,0:T(8,128)(2,1)} %get-tuple-element.37), channel_id=1, source_target_pairs={{0,16},{1,17},{2,18},{3,19},{16,0},{17,1},{18,2},{19,3},{4,20},{5,... | collective-permute-start | bytes 245768 | tf_op jit(solution)/shard_map/ppermute | solution.py:436
  7.9 11.3 %collective-permute-start.5 = (bf16[32,1280]{1,0:T(8,128)(2,1)}, bf16[32,1280]{1,0:T(8,128)(2,1)S(1)}, u32[]{:S(2)}, u32[]{:S(2)}) collective-permute-start(bf16[32,1280]{1,0:T(8,128)(2,1)} %get-tuple-element.41), channel_id=1, source_target_pairs={{0,2},{1,3},{2,0},{3,1},{16,18},{17,19},{18,16},{19,17},{4,6},{5,7... | collective-permute-start | bytes 245768 | tf_op jit(solution)/shard_map/ppermute | solution.py:436
  8.9 11.5 %collective-permute-start.8 = (bf16[32,1280]{1,0:T(8,128)(2,1)}, bf16[32,1280]{1,0:T(8,128)(2,1)S(1)}, u32[]{:S(2)}, u32[]{:S(2)}) collective-permute-start(bf16[32,1280]{1,0:T(8,128)(2,1)} %get-tuple-element.42), channel_id=1, source_target_pairs={{0,18},{1,19},{2,16},{3,17},{16,2},{17,3},{18,0},{19,1},{4,22},{5,... | collective-permute-start | bytes 245768 | tf_op jit(solution)/shard_map/ppermute | solution.py:436
  10.5 10.4 %collective-permute-start.11 = (bf16[32,1280]{1,0:T(8,128)(2,1)}, bf16[32,1280]{1,0:T(8,128)(2,1)S(1)}, u32[]{:S(2)}, u32[]{:S(2)}) collective-permute-start(bf16[32,1280]{1,0:T(8,128)(2,1)} %get-tuple-element.46), channel_id=1, source_target_pairs={{0,1},{1,0},{2,3},{3,2},{16,17},{17,16},{18,19},{19,18},{4,5},{5,4... | collective-permute-start | bytes 245768 | tf_op jit(solution)/shard_map/ppermute | solution.py:436
  16.0 7.0 %collective-permute-start.12 = (bf16[32,1280]{1,0:T(8,128)(2,1)}, bf16[32,1280]{1,0:T(8,128)(2,1)S(1)}, u32[]{:S(2)}, u32[]{:S(2)}) collective-permute-start(bf16[32,1280]{1,0:T(8,128)(2,1)} %get-tuple-element.47), channel_id=1, source_target_pairs={{0,3},{1,2},{2,1},{3,0},{16,19},{17,18},{18,17},{19,16},{4,7},{5,6... | collective-permute-start | bytes 245768 | tf_op jit(solution)/shard_map/ppermute | solution.py:436
  17.9 6.4 %collective-permute-start = (bf16[1,1,32,1280]{3,2,1,0:T(8,128)(2,1)}, bf16[1,1,32,1280]{3,2,1,0:T(8,128)(2,1)S(1)}, u32[]{:S(2)}, u32[]{:S(2)}) collective-permute-start(bf16[1,1,32,1280]{3,2,1,0:T(8,128)(2,1)} %bitcast.21), channel_id=1, source_target_pairs={{0,4},{4,0},{8,12},{12,8},{1,5},{5,1},{9,13},{13,9},{2,6},{6,2},{1... | collective-permute-start | bytes 245768 | tf_op jit(solution)/shard_map/ppermute | solution.py:440
  19.2 11.8 %collective-permute-start.3 = (bf16[1,1,32,1280]{3,2,1,0:T(8,128)(2,1)S(1)}, bf16[1,1,32,1280]{3,2,1,0:T(8,128)(2,1)S(1)}, u32[]{:S(2)}, u32[]{:S(2)}) collective-permute-start(bf16[1,1,32,1280]{3,2,1,0:T(8,128)(2,1)S(1)} %bitcast.19), channel_id=1, source_target_pairs={{0,8},{4,12},{8,0},{12,4},{1,9},{5,13},{9,1},{13,5},{2,10},{6,14},... | collective-permute-start | bytes 245768 | tf_op jit(solution)/shard_map/ppermute | solution.py:440
  20.4 6.4 %collective-permute-start.6 = (bf16[1,1,32,1280]{3,2,1,0:T(8,128)(2,1)S(1)}, bf16[1,1,32,1280]{3,2,1,0:T(8,128)(2,1)S(1)}, u32[]{:S(2)}, u32[]{:S(2)}) collective-permute-start(bf16[1,1,32,1280]{3,2,1,0:T(8,128)(2,1)S(1)} %bitcast.23), channel_id=1, source_target_pairs={{0,4},{4,0},{8,12},{12,8},{1,5},{5,1},{9,13},{13,9},{2,6},{6,2},{1... | collective-permute-start | bytes 245768 | tf_op jit(solution)/shard_map/ppermute | solution.py:440
  20.9 5.6 %collective-permute-start.9 = (bf16[1,1,32,1280]{3,2,1,0:T(8,128)(2,1)S(1)}, bf16[1,1,32,1280]{3,2,1,0:T(8,128)(2,1)S(1)}, u32[]{:S(2)}, u32[]{:S(2)}) collective-permute-start(bf16[1,1,32,1280]{3,2,1,0:T(8,128)(2,1)S(1)} %bitcast.25), channel_id=1, source_target_pairs={{0,8},{4,12},{8,0},{12,4},{1,9},{5,13},{9,1},{13,5},{2,10},{6,14},... | collective-permute-start | bytes 245768 | tf_op jit(solution)/shard_map/ppermute | solution.py:440
  23.0 6.4 %collective-permute-start.17 = (bf16[1,2,32,1280]{3,2,1,0:T(8,128)(2,1)S(1)}, bf16[1,2,32,1280]{3,2,1,0:T(8,128)(2,1)S(1)}, u32[]{:S(2)}, u32[]{:S(2)}) collective-permute-start(bf16[1,2,32,1280]{3,2,1,0:T(8,128)(2,1)S(1)} %maximum_bitcast_fusion.1), channel_id=1, source_target_pairs={{0,8},{4,12},{8,0},{12,4},{1,9},{5,13},{9,1},{13,5},{2,10},{6,14},... | collective-permute-start | bytes 491528 | tf_op jit(solution)/shard_map/ppermute | solution.py:440
  24.3 5.1 %collective-permute-start.13 = (bf16[1,2,32,1280]{3,2,1,0:T(8,128)(2,1)S(1)}, bf16[1,2,32,1280]{3,2,1,0:T(8,128)(2,1)S(1)}, u32[]{:S(2)}, u32[]{:S(2)}) collective-permute-start(bf16[1,2,32,1280]{3,2,1,0:T(8,128)(2,1)S(1)} %maximum_bitcast_fusion), channel_id=1, source_target_pairs={{0,4},{4,0},{8,12},{12,8},{1,5},{5,1},{9,13},{13,9},{2,6},{6,2},{1... | collective-permute-start | bytes 491528 | tf_op jit(solution)/shard_map/ppermute | solution.py:440
  26.5 12.4 %collective-permute-start.1 = (bf16[2,1,32,1280]{3,2,1,0:T(8,128)(2,1)S(1)}, bf16[2,1,32,1280]{3,2,1,0:T(8,128)(2,1)}, u32[]{:S(2)}, u32[]{:S(2)}) collective-permute-start(bf16[2,1,32,1280]{3,2,1,0:T(8,128)(2,1)S(1)} %pad_maximum_fusion.2.refs_0_), channel_id=1, source_target_pairs={{0,8},{4,12},{8,0},{12,4},{1,9},{5,13},{9,1},{13,5},{2,10},{6,14},... | collective-permute-start | bytes 491528 | tf_op jit(solution)/shard_map/ppermute | solution.py:440
  26.8 6.2 %collective-permute-start.10 = (bf16[2,1,32,1280]{3,2,1,0:T(8,128)(2,1)S(1)}, bf16[2,1,32,1280]{3,2,1,0:T(8,128)(2,1)S(1)}, u32[]{:S(2)}, u32[]{:S(2)}) collective-permute-start(bf16[2,1,32,1280]{3,2,1,0:T(8,128)(2,1)S(1)} %pad_maximum_fusion.5.refs_2_), channel_id=1, source_target_pairs={{0,4},{4,0},{8,12},{12,8},{1,5},{5,1},{9,13},{13,9},{2,6},{6,2},{1... | collective-permute-start | bytes 491528 | tf_op jit(solution)/shard_map/ppermute | solution.py:440
  29.4 6.1 %collective-permute-start.7 = (bf16[2,1,32,1280]{3,2,1,0:T(8,128)(2,1)}, bf16[2,1,32,1280]{3,2,1,0:T(8,128)(2,1)}, u32[]{:S(2)}, u32[]{:S(2)}) collective-permute-start(bf16[2,1,32,1280]{3,2,1,0:T(8,128)(2,1)} %pad_maximum_fusion.4.refs_0_), channel_id=1, source_target_pairs={{0,8},{4,12},{8,0},{12,4},{1,9},{5,13},{9,1},{13,5},{2,10},{6,14},... | collective-permute-start | bytes 491528 | tf_op jit(solution)/shard_map/ppermute | solution.py:440
  29.5 15.9 %collective-permute-start.14 = (bf16[2,2,32,1280]{3,2,1,0:T(8,128)(2,1)S(1)}, bf16[2,2,32,1280]{3,2,1,0:T(8,128)(2,1)}, u32[]{:S(2)}, u32[]{:S(2)}) collective-permute-start(bf16[2,2,32,1280]{3,2,1,0:T(8,128)(2,1)S(1)} %pad_maximum_fusion.refs_6_), channel_id=1, source_target_pairs={{0,8},{4,12},{8,0},{12,4},{1,9},{5,13},{9,1},{13,5},{2,10},{6,14},... | collective-permute-start | bytes 983048 | tf_op jit(solution)/shard_map/ppermute | solution.py:440
  31.0 14.4 %collective-permute-start.18 = (bf16[2,2,32,1280]{3,2,1,0:T(8,128)(2,1)S(1)}, bf16[2,2,32,1280]{3,2,1,0:T(8,128)(2,1)}, u32[]{:S(2)}, u32[]{:S(2)}) collective-permute-start(bf16[2,2,32,1280]{3,2,1,0:T(8,128)(2,1)S(1)} %pad_maximum_fusion.1.refs_8_), channel_id=1, source_target_pairs={{0,4},{4,0},{8,12},{12,8},{1,5},{5,1},{9,13},{13,9},{2,6},{6,2},{1... | collective-permute-start | bytes 983048 | tf_op jit(solution)/shard_map/ppermute | solution.py:440
  33.0 0.7 copy-start.2
  33.7 9.2 %collective-permute-start.4 = (bf16[2,1,32,1280]{3,2,1,0:T(8,128)(2,1)}, bf16[2,1,32,1280]{3,2,1,0:T(8,128)(2,1)}, u32[]{:S(2)}, u32[]{:S(2)}) collective-permute-start(bf16[2,1,32,1280]{3,2,1,0:T(8,128)(2,1)} %pad_maximum_fusion.3.refs_2_), channel_id=1, source_target_pairs={{0,4},{4,0},{8,12},{12,8},{1,5},{5,1},{9,13},{13,9},{2,6},{6,2},{1... | collective-permute-start | bytes 491528 | tf_op jit(solution)/shard_map/ppermute | solution.py:440
  35.5 0.9 %copy-start.3 = (bf16[2,1,32,1280]{3,2,1,0:T(8,128)(2,1)S(1)}, bf16[2,1,32,1280]{3,2,1,0:T(8,128)(2,1)}, u32[]{:S(2)}) copy-start(bf16[2,1,32,1280]{3,2,1,0:T(8,128)(2,1)} %copy-done.2) | copy-start | bytes 491524
  36.5 8.9 %copy-start.7 = (s32[1,8]{1,0:T(1,128)S(1)}, s32[1,8]{1,0:T(1,128)}, u32[]{:S(2)}) copy-start(s32[1,8]{1,0:T(1,128)} %req_ref.3) | copy-start | bytes 100
  55.1 30.1 %copy-start.1 = (bf16[128,1280]{1,0:T(8,128)(2,1)S(1)}, bf16[128,1280]{1,0:T(8,128)(2,1)}, u32[]{:S(2)}) copy-start(bf16[128,1280]{1,0:T(8,128)(2,1)} %get-tuple-element.33.moved_ref) | copy-start | bytes 983044
  55.1 30.1 %copy-start.5 = (bf16[128,128]{1,0:T(8,128)(2,1)S(1)}, bf16[128,128]{1,0:T(8,128)(2,1)}, u32[]{:S(2)}) copy-start(bf16[128,128]{1,0:T(8,128)(2,1)} %get-tuple-element.34.lo_ref) | copy-start | bytes 98308
  55.1 30.1 %copy-start.6 = (bf16[128,128]{1,0:T(8,128)(2,1)S(1)}, bf16[128,128]{1,0:T(8,128)(2,1)}, u32[]{:S(2)}) copy-start(bf16[128,128]{1,0:T(8,128)(2,1)} %get-tuple-element.35.hi_ref) | copy-start | bytes 98308
  55.1 3.4 %collective-permute-start.19 = (bf16[4,16,640]{2,1,0:T(8,128)(2,1)S(1)}, bf16[4,16,640]{2,1,0:T(8,128)(2,1)S(1)}, u32[]{:S(2)}, u32[]{:S(2)}) collective-permute-start(bf16[4,16,640]{2,1,0:T(8,128)(2,1)S(1)} %get-tuple-element.54), channel_id=1, source_target_pairs={{0,4},{4,0},{8,12},{12,8},{1,5},{5,1},{9,13},{13,9},{2,6},{6,2},{1... | collective-permute-start | bytes 245768 | tf_op jit(solution)/shard_map/ppermute | solution.py:440
  55.2 5.4 %collective-permute-start.20 = (bf16[4,16,640]{2,1,0:T(8,128)(2,1)S(1)}, bf16[4,16,640]{2,1,0:T(8,128)(2,1)S(1)}, u32[]{:S(2)}, u32[]{:S(2)}) collective-permute-start(bf16[4,16,640]{2,1,0:T(8,128)(2,1)S(1)} %get-tuple-element.55), channel_id=1, source_target_pairs={{0,8},{4,12},{8,0},{12,4},{1,9},{5,13},{9,1},{13,5},{2,10},{6,14},... | collective-permute-start | bytes 245768 | tf_op jit(solution)/shard_map/ppermute | solution.py:440
  55.7 4.9 %collective-permute-start.21 = (bf16[4,16,640]{2,1,0:T(8,128)(2,1)S(1)}, bf16[4,16,640]{2,1,0:T(8,128)(2,1)S(1)}, u32[]{:S(2)}, u32[]{:S(2)}) collective-permute-start(bf16[4,16,640]{2,1,0:T(8,128)(2,1)S(1)} %get-tuple-element.56), channel_id=1, source_target_pairs={{0,12},{4,8},{8,4},{12,0},{1,13},{5,9},{9,5},{13,1},{2,14},{6,10},... | collective-permute-start | bytes 245768 | tf_op jit(solution)/shard_map/ppermute | solution.py:440
  57.9 9.0 %collective-permute-start.25 = (bf16[4,16,640]{2,1,0:T(8,128)(2,1)S(1)}, bf16[4,16,640]{2,1,0:T(8,128)(2,1)S(1)}, u32[]{:S(2)}, u32[]{:S(2)}) collective-permute-start(bf16[4,16,640]{2,1,0:T(8,128)(2,1)S(1)} %get-tuple-element.58), channel_id=1, source_target_pairs={{0,4},{4,0},{8,12},{12,8},{1,5},{5,1},{9,13},{13,9},{2,6},{6,2},{1... | collective-permute-start | bytes 245768 | tf_op jit(solution)/shard_map/ppermute | solution.py:440
  57.9 9.6 %collective-permute-start.26 = (bf16[4,16,640]{2,1,0:T(8,128)(2,1)S(1)}, bf16[4,16,640]{2,1,0:T(8,128)(2,1)S(1)}, u32[]{:S(2)}, u32[]{:S(2)}) collective-permute-start(bf16[4,16,640]{2,1,0:T(8,128)(2,1)S(1)} %get-tuple-element.59), channel_id=1, source_target_pairs={{0,8},{4,12},{8,0},{12,4},{1,9},{5,13},{9,1},{13,5},{2,10},{6,14},... | collective-permute-start | bytes 245768 | tf_op jit(solution)/shard_map/ppermute | solution.py:440
  58.5 9.1 %collective-permute-start.27 = (bf16[4,16,640]{2,1,0:T(8,128)(2,1)S(1)}, bf16[4,16,640]{2,1,0:T(8,128)(2,1)S(1)}, u32[]{:S(2)}, u32[]{:S(2)}) collective-permute-start(bf16[4,16,640]{2,1,0:T(8,128)(2,1)S(1)} %get-tuple-element.60), channel_id=1, source_target_pairs={{0,12},{4,8},{8,4},{12,0},{1,13},{5,9},{9,5},{13,1},{2,14},{6,10},... | collective-permute-start | bytes 245768 | tf_op jit(solution)/shard_map/ppermute | solution.py:440
  60.7 10.8 %collective-permute-start.22 = (bf16[4,16,640]{2,1,0:T(8,128)(2,1)S(1)}, bf16[4,16,640]{2,1,0:T(8,128)(2,1)S(1)}, u32[]{:S(2)}, u32[]{:S(2)}) collective-permute-start(bf16[4,16,640]{2,1,0:T(8,128)(2,1)S(1)} %pad_maximum_fusion.7), channel_id=1, source_target_pairs={{0,16},{1,17},{2,18},{3,19},{16,0},{17,1},{18,2},{19,3},{4,20},{5,... | collective-permute-start | bytes 245768 | tf_op jit(solution)/shard_map/ppermute | solution.py:436
  65.4 6.4 %collective-permute-start.23 = (bf16[4,16,640]{2,1,0:T(8,128)(2,1)S(1)}, bf16[4,16,640]{2,1,0:T(8,128)(2,1)S(1)}, u32[]{:S(2)}, u32[]{:S(2)}) collective-permute-start(bf16[4,16,640]{2,1,0:T(8,128)(2,1)S(1)} %pad_maximum_fusion.8), channel_id=1, source_target_pairs={{0,1},{1,0},{2,3},{3,2},{16,17},{17,16},{18,19},{19,18},{4,5},{5,4... | collective-permute-start | bytes 245768 | tf_op jit(solution)/shard_map/ppermute | solution.py:436
  66.9 6.2 %collective-permute-start.24 = (bf16[4,16,640]{2,1,0:T(8,128)(2,1)S(1)}, bf16[4,16,640]{2,1,0:T(8,128)(2,1)S(1)}, u32[]{:S(2)}, u32[]{:S(2)}) collective-permute-start(bf16[4,16,640]{2,1,0:T(8,128)(2,1)S(1)} %pad_maximum_fusion.9), channel_id=1, source_target_pairs={{0,17},{1,16},{2,19},{3,18},{16,1},{17,0},{18,3},{19,2},{4,21},{5,... | collective-permute-start | bytes 245768 | tf_op jit(solution)/shard_map/ppermute | solution.py:436
  67.6 6.0 %collective-permute-start.28 = (bf16[4,16,640]{2,1,0:T(8,128)(2,1)S(1)}, bf16[4,16,640]{2,1,0:T(8,128)(2,1)S(1)}, u32[]{:S(2)}, u32[]{:S(2)}) collective-permute-start(bf16[4,16,640]{2,1,0:T(8,128)(2,1)S(1)} %pad_maximum_fusion.10), channel_id=1, source_target_pairs={{0,2},{1,3},{2,0},{3,1},{16,18},{17,19},{18,16},{19,17},{4,6},{5,7... | collective-permute-start | bytes 245768 | tf_op jit(solution)/shard_map/ppermute | solution.py:436
  69.5 10.2 %collective-permute-start.29 = (bf16[4,16,640]{2,1,0:T(8,128)(2,1)S(1)}, bf16[4,16,640]{2,1,0:T(8,128)(2,1)S(1)}, u32[]{:S(2)}, u32[]{:S(2)}) collective-permute-start(bf16[4,16,640]{2,1,0:T(8,128)(2,1)S(1)} %pad_maximum_fusion.11), channel_id=1, source_target_pairs={{0,18},{1,19},{2,16},{3,17},{16,2},{17,3},{18,0},{19,1},{4,22},{5,... | collective-permute-start | bytes 245768 | tf_op jit(solution)/shard_map/ppermute | solution.py:436
  71.4 11.1 %collective-permute-start.30 = (bf16[4,16,640]{2,1,0:T(8,128)(2,1)S(1)}, bf16[4,16,640]{2,1,0:T(8,128)(2,1)S(1)}, u32[]{:S(2)}, u32[]{:S(2)}) collective-permute-start(bf16[4,16,640]{2,1,0:T(8,128)(2,1)S(1)} %pad_maximum_fusion.12), channel_id=1, source_target_pairs={{0,3},{1,2},{2,1},{3,0},{16,19},{17,18},{18,17},{19,16},{4,7},{5,6... | collective-permute-start | bytes 245768 | tf_op jit(solution)/shard_map/ppermute | solution.py:436
  71.8 13.4 %collective-permute-start.31 = (bf16[4,16,640]{2,1,0:T(8,128)(2,1)S(1)}, bf16[4,16,640]{2,1,0:T(8,128)(2,1)S(1)}, u32[]{:S(2)}, u32[]{:S(2)}) collective-permute-start(bf16[4,16,640]{2,1,0:T(8,128)(2,1)S(1)} %pad_maximum_fusion.13), channel_id=1, source_target_pairs={{0,19},{1,18},{2,17},{3,16},{16,3},{17,2},{18,1},{19,0},{4,23},{5,... | collective-permute-start | bytes 245768 | tf_op jit(solution)/shard_map/ppermute | solution.py:436
